TPU v7x, 512 devices: a whole 4x4x16 slice. The times are simulated.
512 devices in a mesh: rows: 128 (over z, x, y_lo), cols: 4 (over y_hi, core).
Axes of the slice: x: 4, y: 4 (y_hi: 2, y_lo: 2; y = y_hi * 2 + y_lo), z: 16, core: 2. Of those that a mesh axis runs over, the one named last changes fastest.
Arguments:
- events: float32 [32768, 16384], P('rows', 'cols'), may hold values from -520 to 520
- sample_mask: int32 [32768, 128], P('rows', 'cols'), may hold values from 0 to 1, as said below
- keep_rate: float32 [128], P('cols'), may hold values from 0.25 to 1, as said below
Outputs:
- similarity: float32 [256, 16384], P('rows', 'cols')
Inputs may be any that keep to these rules, and one draw needn't show every extreme that they name: `sample_mask`: each entry is 1 with probability keep_rate of its block, independently of all others. `keep_rate`: multiples of 1/1024.
All inputs are finite; a program needn't handle non-finite values.
Results may differ from a plain program's by a relative error of at most 0.0001.
Values sent between devices are 32-bit elements; how exact they have to be, the bound alone decides.
No kernel may reach another device: no remote copies, remote signals or barrier semaphores. Data moves between devices by JAX's collectives and lax.ppermute only.
A program may use at most 64 MiB of HBM per device.

v0:
```python
import math

import jax
import jax.numpy as jnp
from jax import lax
from jax.sharding import Mesh
from jax.sharding import PartitionSpec as P

QUERY_GROUP = 64
ROWS = ("rows_0", "rows_1", "rows_2")


epsilon = 1e-06


def rows_first(arrays, axis, dims):
    turned = [jnp.moveaxis(a, dim, 0) for a, dim in zip(arrays, dims)]
    widths = [t[0].size for t in turned]
    both = jnp.concatenate([t.reshape(-1, w) for t, w in zip(turned, widths)], axis=1)
    result = lax.all_gather(both, axis, axis=0, tiled=True)
    parts = jnp.split(result, [sum(widths[:k]) for k in range(1, len(widths))], axis=1)
    return tuple(
        (
            jnp.moveaxis(b.reshape(-1, *t.shape[1:]), 0, dim)
            for b, t, dim in zip(parts, turned, dims)
        )
    )


def sent_to_all(shard, axis):
    copies = jnp.broadcast_to(shard, (lax.axis_size(axis), *shard.shape))
    return lax.all_to_all(copies, axis, split_axis=0, concat_axis=0, tiled=True)


def taken_together(shard, axis):
    return sent_to_all(shard, axis).sum(axis=0)


def over_axes(shard, axes):
    far, near = axes
    return taken_together(taken_together(shard, near), far)


def packed_total(arrays, axis):
    ends = [0]
    for a in arrays:
        ends.append(ends[-1] + a.size)
    subtotal = over_axes(jnp.concatenate([a.ravel() for a in arrays]), axis)
    return tuple((subtotal[b:e].reshape(a.shape) for a, b, e in zip(arrays, ends, ends[1:])))


def in_blocks(shard, dim, count):
    before, after = (shard.shape[:dim], shard.shape[dim + 1 :])
    return jnp.moveaxis(shard.reshape(*before, count, -1, *after), dim, 0)


def summed_on_arrival(shard, axis, dim):
    parts = in_blocks(shard, dim, lax.axis_size(axis))
    arrived = lax.all_to_all(parts, axis, split_axis=0, concat_axis=0, tiled=True)
    return arrived.sum(axis=0)


def summed_rows(shard, axes, dim):
    far, near = axes
    parts = in_blocks(shard, dim, lax.axis_size(far))
    nearer = summed_on_arrival(parts, near, dim + 1)
    arrived = lax.all_to_all(nearer, far, split_axis=0, concat_axis=0, tiled=True)
    return arrived.sum(axis=0)


def widen_blocks(values):
    spread = jnp.broadcast_to(values[..., None], values.shape + (128,))
    return spread.reshape(values.shape[:-1] + (values.shape[-1] * 128,))


def transposed_product(left, right):
    return lax.dot_general(
        left,
        right,
        (((0,), (0,)), ((), ())),
        precision=lax.Precision.HIGHEST,
        preferred_element_type=jnp.float32,
    )


def shards(events, sample_mask, keep_rate):
    row_count, width = events.shape
    blocks = sample_mask.shape[1]
    keeping = sample_mask.astype(jnp.float32)[:, :, None]
    sampled = (events.reshape(row_count, blocks, 128) * keeping).reshape(row_count, width)
    local_squares = jnp.sum(events * events, axis=0)
    rates = widen_blocks(keep_rate)
    picked = sampled[:, :QUERY_GROUP]
    queries, query_part, query_rate = rows_first(
        (picked, local_squares[None, :QUERY_GROUP], rates[None, :QUERY_GROUP]), "cols", (1, 1, 1)
    )
    devices = lax.axis_size(ROWS)
    factor = math.sqrt(row_count * devices)
    count = queries.shape[1]
    share = count // devices
    place = lax.axis_index(ROWS)
    column_squares, query_squares = packed_total(
        (local_squares, query_part[0]), ("rows_0", ("rows_1", "rows_2"))
    )
    gram = summed_rows(transposed_product(queries, sampled), (("rows_0", "rows_1"), "rows_2"), 0)
    owned = lax.dynamic_slice_in_dim(query_squares * query_rate[0], place * share, share)
    query_weight = lax.rsqrt(owned + epsilon)
    column_weight = lax.rsqrt(column_squares * rates + epsilon)
    return factor * query_weight[:, None] * gram * column_weight[None, :]


def solution(mesh):
    torus = Mesh(
        mesh.devices.reshape(16, 4, 2, mesh.shape["cols"]), ("rows_0", "rows_1", "rows_2", "cols")
    )
    return jax.shard_map(
        shards,
        mesh=torus,
        in_specs=(P(ROWS, "cols"), P(ROWS, "cols"), P("cols")),
        out_specs=P(ROWS, "cols"),
        check_vma=False,
    )
```

profile of v0, /device:TPU:2, one launch (start us, length us, event | category | flops | bytes accessed | tf_op | source)
XLA Modules:
  0.0 236.3 jit_solution(12675952503954246235)
XLA Ops:
  0.0 5.6 %copy.30 = f32[256,4096]{0,1:T(8,128)} copy(f32[256,4096]{1,0:T(8,128)} %param.3) | data formatting | bytes 8388608 | tf_op args[0]
  5.6 2.7 %multiply_reduce_fusion = f32[4096]{0:T(1024)S(1)} fusion(f32[256,4096]{1,0:T(8,128)} %param.3), kind=kLoop, calls=%fused_computation.3 | loop fusion | flops 2093056 | bytes 4210688 | tf_op jit(solution)/shard_map/reduce_sum | solution.py:91
  8.3 0.7 copy-done.1
  9.1 0.3 bitcast_multiply_fusion
  9.4 2.0 copy-done
  11.7 8.1 %all_gather.3 = f32[256,258]{1,0:T(8,128)S(1)} all-gather(f32[64,258]{1,0:T(8,128)S(1)} %pad_maximum_fusion), channel_id=1, replica_groups=mesh['rows_0'=16,'rows_1'=4,'rows_2'=2,'cols'=4] {'cols'}, dimensions={0}, use_global_device_ids=true | all-gather | bytes 330240 | tf_op jit(solution)/shard_map/all_gather | solution.py:20
  19.9 0.2 slice_reduce_fusion.1
  20.1 0.7 broadcast_in_dim.7
  20.8 8.7 %all-to-all-start = ((f32[8,1,4352]{2,1,0:T(1,128)}), f32[8,1,4352]{2,1,0:T(1,128)S(1)}, u32[]{:S(2)}, u32[]{:S(2)}) async-start(f32[8,1,4352]{2,1,0:T(1,128)} %broadcast_in_dim.7), calls=%async_computation | async-start | bytes 278528 | tf_op jit(solution)/shard_map/all_to_all | solution.py:32
  29.5 0.1 dot_general.5
  29.7 12.5 %convolution_bitcast_fusion = f32[2,64,2,4096]{3,1,2,0:T(8,128)} fusion(f32[256,4096]{0,1:T(8,128)} %copy-done, f32[64,2,2,256]{3,2,1,0:T(2,128)S(1)} %dot_general.5), kind=kOutput, calls=%fused_computation | convolution fusion | flops 3221225472 | bytes 8650752 | tf_op jit(solution)/shard_map/dot_general | solution.py:77
  42.1 5.6 %all-to-all-start.2 = ((f32[2,64,2,4096]{3,1,2,0:T(8,128)}), f32[2,64,2,4096]{3,1,2,0:T(8,128)}, u32[]{:S(2)}, u32[]{:S(2)}) async-start(f32[2,64,2,4096]{3,1,2,0:T(8,128)} %convolution_bitcast_fusion), calls=%async_computation.2 | async-start | bytes 8388608 | tf_op jit(solution)/shard_map/all_to_all | solution.py:59
  47.7 0.1 reduce_sum.46
  47.8 47.8 %all-to-all-done.2 = f32[2,64,2,4096]{3,1,2,0:T(8,128)} async-done(((f32[2,64,2,4096]{3,1,2,0:T(8,128)}), f32[2,64,2,4096]{3,1,2,0:T(8,128)}, u32[]{:S(2)}, u32[]{:S(2)}) %all-to-all-start.2) | async-done | bytes 4194336 | tf_op jit(solution)/shard_map/all_to_all | solution.py:59
  95.6 0.9 broadcast_in_dim.8
  96.5 11.6 %all-to-all-start.1 = ((f32[16,1,4352]{2,1,0:T(1,128)}), f32[16,1,4352]{2,1,0:T(1,128)S(1)}, u32[]{:S(2)}, u32[]{:S(2)}) async-start(f32[16,1,4352]{2,1,0:T(1,128)} %broadcast_in_dim.8), calls=%async_computation.1 | async-start | bytes 557056 | tf_op jit(solution)/shard_map/all_to_all | solution.py:32
  108.1 2.7 %reduce_sum.48 = f32[64,2,4096]{2,0,1:T(8,128)S(1)} reduce(f32[2,64,2,4096]{3,1,2,0:T(8,128)} %all-to-all-done.2, f32[]{:T(128)} %constant.12.clone.1), dimensions={0}, to_apply=%region_3.0 | reduce | flops 524288 | bytes 6291460 | tf_op jit(solution)/shard_map/reduce_sum | solution.py:60
  110.8 3.0 %copy.37 = f32[64,2,4096]{2,1,0:T(2,128)} copy(f32[64,2,4096]{2,0,1:T(8,128)S(1)} %reduce_sum.48) | data formatting | bytes 4194304 | tf_op jit(solution)/shard_map/reduce_sum | solution.py:60
  113.7 12.6 %all-to-all-done.1 = f32[16,1,4352]{2,1,0:T(1,128)S(1)} async-done(((f32[16,1,4352]{2,1,0:T(1,128)}), f32[16,1,4352]{2,1,0:T(1,128)S(1)}, u32[]{:S(2)}, u32[]{:S(2)}) %all-to-all-start.1) | async-done | bytes 278560 | tf_op jit(solution)/shard_map/all_to_all | solution.py:32
  126.3 9.1 %all-to-all-start.3 = ((f32[64,2,4096]{2,1,0:T(2,128)}), f32[64,2,4096]{2,1,0:T(2,128)S(1)}, u32[]{:S(2)}, u32[]{:S(2)}) async-start(f32[64,2,4096]{2,1,0:T(2,128)} %copy.37), calls=%async_computation.3 | async-start | bytes 4194304 | tf_op jit(solution)/shard_map/all_to_all | solution.py:67
  135.4 0.2 reduce_sum.47
  135.8 99.1 %all-to-all-done.3 = f32[64,2,4096]{2,1,0:T(2,128)S(1)} async-done(((f32[64,2,4096]{2,1,0:T(2,128)}), f32[64,2,4096]{2,1,0:T(2,128)S(1)}, u32[]{:S(2)}, u32[]{:S(2)}) %all-to-all-start.3) | async-done | bytes 2097184 | tf_op jit(solution)/shard_map/all_to_all | solution.py:67
  234.9 0.7 reduce_sum.49
  235.6 0.7 multiply_multiply_fusion
  (20 shorter events, 0.6 us)
Async XLA Ops:
  0.0 8.3 %copy-start.2 = (s32[256,32]{0,1:T(8,128)S(1)}, s32[256,32]{0,1:T(8,128)}, u32[]{:S(2)}) copy-start(s32[256,32]{0,1:T(8,128)} %param.4) | copy-start | bytes 98308
  5.6 3.4 %copy-start.1 = (f32[256,4096]{0,1:T(8,128)S(1)}, f32[256,4096]{0,1:T(8,128)}, u32[]{:S(2)}) copy-start(f32[256,4096]{0,1:T(8,128)} %copy.30) | copy-start | bytes 12582916
  9.1 2.4 %copy-start.3 = (f32[32]{0:T(128)S(1)}, f32[32]{0:T(128)}, u32[]{:S(2)}) copy-start(f32[32]{0:T(128)} %param.5) | copy-start | bytes 388
  9.4 2.0 copy-start
  20.8 21.3 %all-to-all-start = ((f32[8,1,4352]{2,1,0:T(1,128)}), f32[8,1,4352]{2,1,0:T(1,128)S(1)}, u32[]{:S(2)}, u32[]{:S(2)}) async-start(f32[8,1,4352]{2,1,0:T(1,128)} %broadcast_in_dim.7), calls=%async_computation | async-start | bytes 278528 | tf_op jit(solution)/shard_map/all_to_all | solution.py:32
  42.1 53.5 %all-to-all-start.2 = ((f32[2,64,2,4096]{3,1,2,0:T(8,128)}), f32[2,64,2,4096]{3,1,2,0:T(8,128)}, u32[]{:S(2)}, u32[]{:S(2)}) async-start(f32[2,64,2,4096]{3,1,2,0:T(8,128)} %convolution_bitcast_fusion), calls=%async_computation.2 | async-start | bytes 8388608 | tf_op jit(solution)/shard_map/all_to_all | solution.py:59
  96.5 29.8 %all-to-all-start.1 = ((f32[16,1,4352]{2,1,0:T(1,128)}), f32[16,1,4352]{2,1,0:T(1,128)S(1)}, u32[]{:S(2)}, u32[]{:S(2)}) async-start(f32[16,1,4352]{2,1,0:T(1,128)} %broadcast_in_dim.8), calls=%async_computation.1 | async-start | bytes 557056 | tf_op jit(solution)/shard_map/all_to_all | solution.py:32
  126.3 108.6 %all-to-all-start.3 = ((f32[64,2,4096]{2,1,0:T(2,128)}), f32[64,2,4096]{2,1,0:T(2,128)S(1)}, u32[]{:S(2)}, u32[]{:S(2)}) async-start(f32[64,2,4096]{2,1,0:T(2,128)} %copy.37), calls=%async_computation.3 | async-start | bytes 4194304 | tf_op jit(solution)/shard_map/all_to_all | solution.py:67
where the time goes:
time: 237 us; the launch traced here: 236 us
  waiting for transfers between devices  159 us (67%)
  starting transfers between devices  35 us (15%)
  local copies, waits for them, and re-layouts  13.6 us (6%)
  matrix products  12.5 us (5%)
  blocking collectives  8.15 us (3%)
  other arithmetic  7.62 us (3%)
    all_to_all x1, waiting for transfers between devices, summed_rows(): lax.all_to_all(nearer, far, split_axis=0, concat_axis=0, tiled=True)  99.1 us
    all_to_all x1, waiting for transfers between devices, summed_on_arrival(): lax.all_to_all(parts, axis, split_axis=0, concat_axis=0, tiled=True)  47.8 us
    all_to_all x2, starting transfers between devices, sent_to_all(): return lax.all_to_all(copies, axis, split_axis=0, concat_axis=0, tiled=True)  20.2 us
    all_to_all x2, waiting for transfers between devices, sent_to_all(): return lax.all_to_all(copies, axis, split_axis=0, concat_axis=0, tiled=True)  12.6 us
    dot_general x1, matrix products, transposed_product(): lax.dot_general(left, right, (((0,), (0,)), ((), ())), precision=lax.Prec...  12.5 us
    all_to_all x1, starting transfers between devices, summed_rows(): lax.all_to_all(nearer, far, split_axis=0, concat_axis=0, tiled=True)  9.13 us
    unnamed x9, local copies, waits for them, and re-layouts  8.32 us
    all_gather x1, blocking collectives, rows_first(): result = lax.all_gather(both, axis, axis=0, tiled=True)  8.15 us
  transfers between devices with their start and end apart: 4, of which 3 were waited for; matrix products, arithmetic and copies ran while one was open for 8% of the time, Pallas kernels for 0%

commit v1 on v0

v1 whole, which is shorter than its diff:
```python
import functools
import math

import jax
import jax.numpy as jnp
from jax import lax
from jax.experimental import pallas as pl
from jax.experimental.pallas import tpu as pltpu
from jax.sharding import Mesh
from jax.sharding import PartitionSpec as P

QUERY_GROUP = 64
BLOCK = 128
Z, X, Y = "rows_0", "rows_1", "rows_2"
ROWS = (Z, X, Y)
PLANE = (X, Y)
EPSILON = 1e-06
CHUNKS = 4


def split(values):
    high = values.astype(jnp.bfloat16)
    low = (values - high.astype(jnp.float32)).astype(jnp.bfloat16)
    return high, low


def gram_kernel(arrived, mask, events, gram, squares, high, low):
    groups, _, rows = arrived.shape
    plane, width = gram.shape[0], events.shape[1]
    step = pl.program_id(0)
    total_blocks = CHUNKS * (width // BLOCK)
    per_group = QUERY_GROUP // plane

    @pl.when(step == 0)
    def _():
        for group in range(groups):
            keep = arrived[group, QUERY_GROUP : QUERY_GROUP + 1, :]
            for place in range(plane):
                part = arrived[group, place * per_group : (place + 1) * per_group, :] * keep
                first = place * groups * per_group + group * per_group
                h, l = split(part)
                high[first : first + per_group, :] = h.astype(jnp.float32)
                low[first : first + per_group, :] = l.astype(jnp.float32)

    values = events[...]
    squares[...] = jnp.sum(values * values, axis=0, keepdims=True)
    blocks = width // BLOCK
    keep = mask[...].astype(jnp.float32)
    keep = jnp.concatenate([keep, jnp.zeros((BLOCK - blocks, rows), jnp.float32)], axis=0).T
    query_high = high[...].astype(jnp.bfloat16)
    query_low = low[...].astype(jnp.bfloat16)
    queries = groups * QUERY_GROUP
    each = queries // plane
    pair = 2 * BLOCK
    for start in range(0, width, pair):
        parts = []
        for at in range(start, start + pair, BLOCK):
            b = at // BLOCK
            parts.append(values[:, at : at + BLOCK] * keep[:, b : b + 1])
        h, l = split(jnp.concatenate(parts, axis=1))
        dot = functools.partial(jnp.dot, preferred_element_type=jnp.float32)
        result = dot(query_high, h) + (dot(query_high, l) + dot(query_low, h))
        for place in range(plane):
            for at in range(0, pair, BLOCK):
                block = step * blocks + (start + at) // BLOCK
                gram[place, pl.ds(block, each, stride=total_blocks), :] = result[
                    place * each : (place + 1) * each, at : at + BLOCK
                ]


def local_gram(arrived, mask, events, plane):
    groups, _, rows = arrived.shape
    queries = groups * QUERY_GROUP
    columns = events.shape[1]
    width = columns // CHUNKS
    shape = (plane, queries // plane * (columns // BLOCK), BLOCK)
    return pl.pallas_call(
        gram_kernel,
        grid=(CHUNKS,),
        in_specs=[
            pl.BlockSpec(arrived.shape, lambda i: (0, 0, 0)),
            pl.BlockSpec((width // BLOCK, rows), lambda i: (i, 0)),
            pl.BlockSpec((rows, width), lambda i: (0, i)),
        ],
        out_specs=[
            pl.BlockSpec(shape, lambda i: (0, 0, 0)),
            pl.BlockSpec((1, width), lambda i: (0, i)),
        ],
        out_shape=[
            jax.ShapeDtypeStruct(shape, jnp.float32),
            jax.ShapeDtypeStruct((1, columns), jnp.float32),
        ],
        scratch_shapes=[pltpu.VMEM((queries, rows), jnp.float32)] * 2,
        compiler_params=pltpu.CompilerParams(
            dimension_semantics=("arbitrary",), vmem_limit_bytes=40 << 20
        ),
        cost_estimate=pl.CostEstimate(
            flops=6 * queries * rows * columns,
            bytes_accessed=4 * (rows * columns + queries * columns),
            transcendentals=0,
        ),
        name="gram",
    )(arrived, mask, events)


def sent_to_all(shard, axis):
    copies = jnp.broadcast_to(shard, (lax.axis_size(axis), *shard.shape))
    return lax.all_to_all(copies, axis, split_axis=0, concat_axis=0, tiled=True)


def summed_by_pairs(value, axis):
    size, apart = lax.axis_size(axis), 1
    while apart < size:
        value = value + lax.ppermute(value, axis, [(i, i ^ apart) for i in range(size)])
        apart *= 2
    return value


def shards(events, sample_mask, keep_rate):
    rows, columns = events.shape
    depth, plane = lax.axis_size(Z), lax.axis_size(X) * lax.axis_size(Y)
    groups = lax.axis_size("cols")
    queries = groups * QUERY_GROUP
    share = queries // (depth * plane)

    mine = events[:, :QUERY_GROUP].reshape(rows, depth // groups, plane, share)
    mine = mine.transpose(2, 1, 3, 0).reshape(QUERY_GROUP, rows)
    keep = sample_mask[:, :1].astype(jnp.float32).T
    rate = jnp.broadcast_to(keep_rate[0], (1, rows))
    extra = jnp.concatenate([keep, rate, jnp.zeros((6, rows), jnp.float32)], axis=0)
    arrived = sent_to_all(jnp.concatenate([mine, extra], axis=0)[None], "cols")
    arrived = arrived.reshape(groups, QUERY_GROUP + 8, rows)

    gram, squares = local_gram(arrived, sample_mask.T, events, plane)
    raw = arrived[:, :QUERY_GROUP].reshape(groups, plane, -1, rows)
    query_squares = jnp.sum(raw * raw, axis=3).transpose(1, 0, 2).reshape(queries)
    query_rate = arrived[:, QUERY_GROUP + 1, 0]

    nearer = lax.all_to_all(gram, PLANE, split_axis=0, concat_axis=0, tiled=True)
    packed = jnp.concatenate([squares.reshape(-1, BLOCK), query_squares.reshape(-1, BLOCK)])
    for axis in (Y, X, Z):
        packed = summed_by_pairs(packed, axis)
    nearer, packed = lax.optimization_barrier((nearer, packed))
    nearer = nearer.sum(axis=0).reshape(depth, share * (columns // BLOCK), BLOCK)
    packed = packed.reshape(1, columns + queries)
    column_squares, query_squares = packed[:, :columns], packed[0, columns:]

    total = lax.all_to_all(nearer, Z, split_axis=0, concat_axis=0, tiled=True).sum(axis=0)
    total = total.reshape(share, columns)

    z, place = lax.axis_index(Z), lax.axis_index(PLANE)
    owned = lax.dynamic_slice_in_dim(query_squares, place * (queries // plane) + z * share, share)
    query_weight = lax.rsqrt(owned * query_rate[z // (depth // groups)] + EPSILON)
    rates = jnp.broadcast_to(keep_rate[:, None], (columns // BLOCK, BLOCK)).reshape(1, columns)
    column_weight = lax.rsqrt(column_squares * rates + EPSILON)
    factor = math.sqrt(rows * depth * plane)
    return factor * query_weight[:, None] * total * column_weight


def solution(mesh):
    torus = Mesh(mesh.devices.reshape(16, 4, 2, mesh.shape["cols"]), (Z, X, Y, "cols"))
    return jax.shard_map(
        shards,
        mesh=torus,
        in_specs=(P(ROWS, "cols"), P(ROWS, "cols"), P("cols")),
        out_specs=P(ROWS, "cols"),
        check_vma=False,
    )
```

time: 237 us -> 175 us (0.74)
  the two profiles are of different devices: /device:TPU:2 before, /device:TPU:8 now
where the time goes in v1:
time: 175 us; the launch traced here: 174 us
  waiting for transfers between devices  81.7 us (47%)
  starting transfers between devices  61.5 us (35%)
  blocking collectives  11.3 us (6%)
  local copies, waits for them, and re-layouts  7.65 us (4%)
  Pallas kernels  6.13 us (4%)
  other arithmetic  5.66 us (3%)
    ppermute x7, waiting for transfers between devices, summed_by_pairs(): lax.ppermute(value, axis, [(i, i ^ apart) for i in range(size)])  61.1 us
    ppermute x7, starting transfers between devices, summed_by_pairs(): lax.ppermute(value, axis, [(i, i ^ apart) for i in range(size)])  40.6 us
    all_to_all x1, waiting for transfers between devices, shards(): lax.all_to_all(nearer, Z, split_axis=0, concat_axis=0, tiled=True)  20.6 us
    all_to_all x1, starting transfers between devices, shards(): lax.all_to_all(nearer, Z, split_axis=0, concat_axis=0, tiled=True)  11.7 us
    all_to_all x1, blocking collectives, sent_to_all(): return lax.all_to_all(copies, axis, split_axis=0, concat_axis=0, tiled=True)  11.3 us
    all_to_all x1, starting transfers between devices, shards(): lax.all_to_all(gram, PLANE, split_axis=0, concat_axis=0, tiled=True)  9.24 us
    pallas_call x1, Pallas kernels, local_gram(): pl.pallas_call(gram_kernel, grid=(CHUNKS,), in_specs=[pl.BlockSpec(arrive...  6.13 us
    unnamed x9, local copies, waits for them, and re-layouts  4.95 us
  transfers between devices with their start and end apart: 9, of which 8 were waited for; matrix products, arithmetic and copies ran while one was open for 1% of the time, Pallas kernels for 0%

profile of v1, /device:TPU:8, one launch (start us, length us, event | category | flops | bytes accessed | tf_op | source)
XLA Modules:
  0.0 174.1 jit_solution(175158172401168631)
XLA Ops:
  1.5 0.9 slice.21
  2.7 11.3 %all_to_all.15 = f32[4,1,72,256]{3,2,1,0:T(8,128)S(1)} all-to-all(f32[4,1,72,256]{3,2,1,0:T(8,128)S(1)} %broadcast_in_dim.19), channel_id=1, replica_groups=mesh['rows_0'=16,'rows_1'=4,'rows_2'=2,'cols'=4] {'cols'}, dimensions={0} | all-to-all | bytes 589824 | tf_op jit(solution)/shard_map/all_to_all | solution.py:108
  14.0 2.2 %copy-done.1 = f32[256,4096]{1,0:T(8,128)S(1)} copy-done((f32[256,4096]{1,0:T(8,128)S(1)}, f32[256,4096]{1,0:T(8,128)}, u32[]{:S(2)}) %copy-start.1) | copy-done | bytes 4194328
  16.2 0.8 copy-done.2
  16.9 6.1 %gram.1 = (f32[8,1024,128]{2,1,0:T(8,128)S(1)}, f32[1,4096]{1,0:T(1,128)S(1)}) custom-call(f32[4,72,256]{2,1,0:T(8,128)S(1)} %bitcast.22, s32[32,256]{1,0:T(8,128)S(1)} %bitcast.27, f32[256,4096]{1,0:T(8,128)S(1)} %copy-done.1), custom_call_target="tpu_custom_call" | custom-call | flops 1610612736 | bytes 8388608 | tf_op jit(solution)/shard_map/gram/pallas_call | solution.py:77
  23.1 2.0 %copy-done = f32[8,1024,128]{2,1,0:T(8,128)} copy-done((f32[8,1024,128]{2,1,0:T(8,128)}, f32[8,1024,128]{2,1,0:T(8,128)S(1)}, u32[]{:S(2)}) %copy-start) | copy-done | bytes 4194328
  25.1 9.2 %all-to-all-start.1 = ((f32[8,1024,128]{2,1,0:T(8,128)}), f32[8,1024,128]{2,1,0:T(8,128)}, u32[]{:S(2)}, u32[]{:S(2)}) async-start(f32[8,1024,128]{2,1,0:T(8,128)} %copy-done), calls=%async_computation.1 | async-start | bytes 8388608 | tf_op jit(solution)/shard_map/all_to_all | solution.py:139
  34.6 2.1 %collective-permute-start = (f32[34,128]{1,0:T(8,128)S(1)}, f32[34,128]{1,0:T(8,128)S(1)}, u32[]{:S(2)}, u32[]{:S(2)}) collective-permute-start(f32[34,128]{1,0:T(8,128)S(1)} %pad_maximum_fusion), channel_id=1, source_target_pairs={{0,4},{4,0},{1,5},{5,1},{2,6},{6,2},{3,7},{7,3},{8,12},{12,8},{9,1... | collective-permute-start | bytes 52232 | tf_op jit(solution)/shard_map/ppermute | solution.py:114
  36.7 32.9 %collective-permute-done = f32[34,128]{1,0:T(8,128)S(1)} collective-permute-done((f32[34,128]{1,0:T(8,128)S(1)}, f32[34,128]{1,0:T(8,128)S(1)}, u32[]{:S(2)}, u32[]{:S(2)}) %collective-permute-start) | collective-permute-done | bytes 17440 | tf_op jit(solution)/shard_map/ppermute | solution.py:114
  69.6 14.1 %collective-permute-start.1 = (f32[34,128]{1,0:T(8,128)S(1)}, f32[34,128]{1,0:T(8,128)S(1)}, u32[]{:S(2)}, u32[]{:S(2)}) collective-permute-start(f32[34,128]{1,0:T(8,128)S(1)} %fusion.3), channel_id=1, source_target_pairs={{0,8},{8,0},{16,24},{24,16},{1,9},{9,1},{17,25},{25,17},{2,10},{10... | collective-permute-start | bytes 52232 | tf_op jit(solution)/shard_map/ppermute | solution.py:114
  83.7 9.4 %collective-permute-done.1 = f32[34,128]{1,0:T(8,128)S(1)} collective-permute-done((f32[34,128]{1,0:T(8,128)S(1)}, f32[34,128]{1,0:T(8,128)S(1)}, u32[]{:S(2)}, u32[]{:S(2)}) %collective-permute-start.1) | collective-permute-done | bytes 17440 | tf_op jit(solution)/shard_map/ppermute | solution.py:114
  93.0 2.4 %collective-permute-start.2 = (f32[34,128]{1,0:T(8,128)S(1)}, f32[34,128]{1,0:T(8,128)S(1)}, u32[]{:S(2)}, u32[]{:S(2)}) collective-permute-start(f32[34,128]{1,0:T(8,128)S(1)} %add.49), channel_id=1, source_target_pairs={{0,16},{8,24},{16,0},{24,8},{1,17},{9,25},{17,1},{25,9},{2,18},{10... | collective-permute-start | bytes 52232 | tf_op jit(solution)/shard_map/ppermute | solution.py:114
  95.4 4.8 %collective-permute-done.2 = f32[34,128]{1,0:T(8,128)S(1)} collective-permute-done((f32[34,128]{1,0:T(8,128)S(1)}, f32[34,128]{1,0:T(8,128)S(1)}, u32[]{:S(2)}, u32[]{:S(2)}) %collective-permute-start.2) | collective-permute-done | bytes 17440 | tf_op jit(solution)/shard_map/ppermute | solution.py:114
  100.2 1.9 %collective-permute-start.3 = (f32[34,128]{1,0:T(8,128)S(1)}, f32[34,128]{1,0:T(8,128)S(1)}, u32[]{:S(2)}, u32[]{:S(2)}) collective-permute-start(f32[34,128]{1,0:T(8,128)S(1)} %add.50), channel_id=1, source_target_pairs={{0,32},{32,0},{64,96},{96,64},{128,160},{160,128},{192,224},{224,1... | collective-permute-start | bytes 52232 | tf_op jit(solution)/shard_map/ppermute | solution.py:114
  102.1 3.7 %collective-permute-done.3 = f32[34,128]{1,0:T(8,128)S(1)} collective-permute-done((f32[34,128]{1,0:T(8,128)S(1)}, f32[34,128]{1,0:T(8,128)S(1)}, u32[]{:S(2)}, u32[]{:S(2)}) %collective-permute-start.3) | collective-permute-done | bytes 17440 | tf_op jit(solution)/shard_map/ppermute | solution.py:114
  105.9 1.9 %collective-permute-start.4 = (f32[34,128]{1,0:T(8,128)S(1)}, f32[34,128]{1,0:T(8,128)S(1)}, u32[]{:S(2)}, u32[]{:S(2)}) collective-permute-start(f32[34,128]{1,0:T(8,128)S(1)} %add.51), channel_id=1, source_target_pairs={{0,64},{32,96},{64,0},{96,32},{128,192},{160,224},{192,128},{224,1... | collective-permute-start | bytes 52232 | tf_op jit(solution)/shard_map/ppermute | solution.py:114
  107.8 4.6 %collective-permute-done.4 = f32[34,128]{1,0:T(8,128)S(1)} collective-permute-done((f32[34,128]{1,0:T(8,128)S(1)}, f32[34,128]{1,0:T(8,128)S(1)}, u32[]{:S(2)}, u32[]{:S(2)}) %collective-permute-start.4) | collective-permute-done | bytes 17440 | tf_op jit(solution)/shard_map/ppermute | solution.py:114
  112.4 6.0 %collective-permute-start.5 = (f32[34,128]{1,0:T(8,128)S(1)}, f32[34,128]{1,0:T(8,128)S(1)}, u32[]{:S(2)}, u32[]{:S(2)}) collective-permute-start(f32[34,128]{1,0:T(8,128)S(1)} %add.52), channel_id=1, source_target_pairs={{0,128},{32,160},{64,192},{96,224},{128,0},{160,32},{192,64},{224,... | collective-permute-start | bytes 52232 | tf_op jit(solution)/shard_map/ppermute | solution.py:114
  118.4 3.6 %collective-permute-done.5 = f32[34,128]{1,0:T(8,128)S(1)} collective-permute-done((f32[34,128]{1,0:T(8,128)S(1)}, f32[34,128]{1,0:T(8,128)S(1)}, u32[]{:S(2)}, u32[]{:S(2)}) %collective-permute-start.5) | collective-permute-done | bytes 17440 | tf_op jit(solution)/shard_map/ppermute | solution.py:114
  122.0 12.2 %collective-permute-start.6 = (f32[34,128]{1,0:T(8,128)S(1)}, f32[34,128]{1,0:T(8,128)S(1)}, u32[]{:S(2)}, u32[]{:S(2)}) collective-permute-start(f32[34,128]{1,0:T(8,128)S(1)} %add.53), channel_id=1, source_target_pairs={{0,256},{32,288},{64,320},{96,352},{128,384},{160,416},{192,448},{... | collective-permute-start | bytes 52232 | tf_op jit(solution)/shard_map/ppermute | solution.py:114
  134.3 2.1 %collective-permute-done.6 = f32[34,128]{1,0:T(8,128)S(1)} collective-permute-done((f32[34,128]{1,0:T(8,128)S(1)}, f32[34,128]{1,0:T(8,128)S(1)}, u32[]{:S(2)}, u32[]{:S(2)}) %collective-permute-start.6) | collective-permute-done | bytes 17440 | tf_op jit(solution)/shard_map/ppermute | solution.py:114
  136.4 3.2 %reduce_sum.31 = f32[1024,128]{1,0:T(8,128)} reduce(f32[8,1024,128]{2,1,0:T(8,128)} %all-to-all-done.1, f32[]{:T(128)} %constant.16.clone.1), dimensions={0}, to_apply=%region_1.0 | reduce | flops 917504 | bytes 4718596 | tf_op jit(solution)/shard_map/reduce_sum | solution.py:144
  139.7 11.7 %all-to-all-start.2 = ((f32[16,64,128]{2,1,0:T(8,128)}), f32[16,64,128]{2,1,0:T(8,128)S(1)}, u32[]{:S(2)}, u32[]{:S(2)}) async-start(f32[16,64,128]{2,1,0:T(8,128)} %bitcast.9), calls=%async_computation.2 | async-start | bytes 1048576 | tf_op jit(solution)/shard_map/all_to_all | solution.py:148
  152.8 20.6 %all-to-all-done.2 = f32[16,64,128]{2,1,0:T(8,128)S(1)} async-done(((f32[16,64,128]{2,1,0:T(8,128)}), f32[16,64,128]{2,1,0:T(8,128)S(1)}, u32[]{:S(2)}, u32[]{:S(2)}) %all-to-all-start.2) | async-done | bytes 524320 | tf_op jit(solution)/shard_map/all_to_all | solution.py:148
  (38 shorter events, 4.2 us)
Async XLA Ops:
  14.0 2.2 %copy-start.1 = (f32[256,4096]{1,0:T(8,128)S(1)}, f32[256,4096]{1,0:T(8,128)}, u32[]{:S(2)}) copy-start(f32[256,4096]{1,0:T(8,128)} %events.1) | copy-start | bytes 12582916
  16.2 0.8 copy-start.2
  23.1 2.0 %copy-start = (f32[8,1024,128]{2,1,0:T(8,128)}, f32[8,1024,128]{2,1,0:T(8,128)S(1)}, u32[]{:S(2)}) copy-start(f32[8,1024,128]{2,1,0:T(8,128)S(1)} %get-tuple-element.9) | copy-start | bytes 12582916
  25.1 111.3 %all-to-all-start.1 = ((f32[8,1024,128]{2,1,0:T(8,128)}), f32[8,1024,128]{2,1,0:T(8,128)}, u32[]{:S(2)}, u32[]{:S(2)}) async-start(f32[8,1024,128]{2,1,0:T(8,128)} %copy-done), calls=%async_computation.1 | async-start | bytes 8388608 | tf_op jit(solution)/shard_map/all_to_all | solution.py:139
  34.3 118.4 %copy-start.3 = (f32[32]{0:T(128)S(1)}, f32[32]{0:T(128)}, u32[]{:S(2)}) copy-start(f32[32]{0:T(128)} %param.5) | copy-start | bytes 388
  34.6 34.9 %collective-permute-start = (f32[34,128]{1,0:T(8,128)S(1)}, f32[34,128]{1,0:T(8,128)S(1)}, u32[]{:S(2)}, u32[]{:S(2)}) collective-permute-start(f32[34,128]{1,0:T(8,128)S(1)} %pad_maximum_fusion), channel_id=1, source_target_pairs={{0,4},{4,0},{1,5},{5,1},{2,6},{6,2},{3,7},{7,3},{8,12},{12,8},{9,1... | collective-permute-start | bytes 52232 | tf_op jit(solution)/shard_map/ppermute | solution.py:114
  69.6 23.5 %collective-permute-start.1 = (f32[34,128]{1,0:T(8,128)S(1)}, f32[34,128]{1,0:T(8,128)S(1)}, u32[]{:S(2)}, u32[]{:S(2)}) collective-permute-start(f32[34,128]{1,0:T(8,128)S(1)} %fusion.3), channel_id=1, source_target_pairs={{0,8},{8,0},{16,24},{24,16},{1,9},{9,1},{17,25},{25,17},{2,10},{10... | collective-permute-start | bytes 52232 | tf_op jit(solution)/shard_map/ppermute | solution.py:114
  93.0 7.2 %collective-permute-start.2 = (f32[34,128]{1,0:T(8,128)S(1)}, f32[34,128]{1,0:T(8,128)S(1)}, u32[]{:S(2)}, u32[]{:S(2)}) collective-permute-start(f32[34,128]{1,0:T(8,128)S(1)} %add.49), channel_id=1, source_target_pairs={{0,16},{8,24},{16,0},{24,8},{1,17},{9,25},{17,1},{25,9},{2,18},{10... | collective-permute-start | bytes 52232 | tf_op jit(solution)/shard_map/ppermute | solution.py:114
  100.2 5.7 %collective-permute-start.3 = (f32[34,128]{1,0:T(8,128)S(1)}, f32[34,128]{1,0:T(8,128)S(1)}, u32[]{:S(2)}, u32[]{:S(2)}) collective-permute-start(f32[34,128]{1,0:T(8,128)S(1)} %add.50), channel_id=1, source_target_pairs={{0,32},{32,0},{64,96},{96,64},{128,160},{160,128},{192,224},{224,1... | collective-permute-start | bytes 52232 | tf_op jit(solution)/shard_map/ppermute | solution.py:114
  105.9 6.6 %collective-permute-start.4 = (f32[34,128]{1,0:T(8,128)S(1)}, f32[34,128]{1,0:T(8,128)S(1)}, u32[]{:S(2)}, u32[]{:S(2)}) collective-permute-start(f32[34,128]{1,0:T(8,128)S(1)} %add.51), channel_id=1, source_target_pairs={{0,64},{32,96},{64,0},{96,32},{128,192},{160,224},{192,128},{224,1... | collective-permute-start | bytes 52232 | tf_op jit(solution)/shard_map/ppermute | solution.py:114
  112.4 9.6 %collective-permute-start.5 = (f32[34,128]{1,0:T(8,128)S(1)}, f32[34,128]{1,0:T(8,128)S(1)}, u32[]{:S(2)}, u32[]{:S(2)}) collective-permute-start(f32[34,128]{1,0:T(8,128)S(1)} %add.52), channel_id=1, source_target_pairs={{0,128},{32,160},{64,192},{96,224},{128,0},{160,32},{192,64},{224,... | collective-permute-start | bytes 52232 | tf_op jit(solution)/shard_map/ppermute | solution.py:114
  122.0 14.4 %collective-permute-start.6 = (f32[34,128]{1,0:T(8,128)S(1)}, f32[34,128]{1,0:T(8,128)S(1)}, u32[]{:S(2)}, u32[]{:S(2)}) collective-permute-start(f32[34,128]{1,0:T(8,128)S(1)} %add.53), channel_id=1, source_target_pairs={{0,256},{32,288},{64,320},{96,352},{128,384},{160,416},{192,448},{... | collective-permute-start | bytes 52232 | tf_op jit(solution)/shard_map/ppermute | solution.py:114
  139.7 33.7 %all-to-all-start.2 = ((f32[16,64,128]{2,1,0:T(8,128)}), f32[16,64,128]{2,1,0:T(8,128)S(1)}, u32[]{:S(2)}, u32[]{:S(2)}) async-start(f32[16,64,128]{2,1,0:T(8,128)} %bitcast.9), calls=%async_computation.2 | async-start | bytes 1048576 | tf_op jit(solution)/shard_map/all_to_all | solution.py:148

commit v2 on v1

v2 whole, which is shorter than its diff:
```python
import functools
import math

import jax
import jax.numpy as jnp
from jax import lax
from jax.experimental import pallas as pl
from jax.experimental.pallas import tpu as pltpu
from jax.sharding import Mesh
from jax.sharding import PartitionSpec as P

QUERY_GROUP = 64
BLOCK = 128
ROWS = ("z", "x", "y")
ALL = ("z", "x", "y", "cols")
DEPTH, WIDTH, PAIR, GROUPS = 16, 4, 2, 4
FAN = 4
FAR = DEPTH // 2
QUERIES = GROUPS * QUERY_GROUP
EXTRA = 40
EPSILON = 1e-06
CHUNKS = 4


def device(z, x, y, c):
    return ((z * WIDTH + x) * PAIR + y) * GROUPS + c


def along_x():
    return {
        c: [
            [device(z, x, y, c) for x in range(WIDTH)]
            for z in range(DEPTH)
            for y in range(PAIR)
        ]
        for c in range(GROUPS)
    }


def along_pairs():
    return {
        c: [
            [device(2 * far + odd, x, y, c) for y in range(PAIR) for odd in range(2)]
            for far in range(FAR)
            for x in range(WIDTH)
        ]
        for c in range(GROUPS)
    }


def stages():
    x, pairs = along_x(), along_pairs()
    first = [g for c in range(GROUPS) for g in (pairs if c % 2 else x)[c]]
    second = [g for c in range(GROUPS) for g in (x if c % 2 else pairs)[c]]
    third = [
        [device(2 * far + odd, x, y, c) for far in range(FAR)]
        for odd in range(2)
        for x in range(WIDTH)
        for y in range(PAIR)
        for c in range(GROUPS)
    ]
    return first, second, third


def split(values):
    high = values.astype(jnp.bfloat16)
    low = (values - high.astype(jnp.float32)).astype(jnp.bfloat16)
    return high, low


def turned(left, right):
    return lax.dot_general(
        left,
        right,
        (((1,), (1,)), ((), ())),
        precision=lax.Precision.HIGHEST,
        preferred_element_type=jnp.float32,
    )


def query_kernel(mask, events, rate, sent):
    rows = events.shape[0]
    n = lax.broadcasted_iota(jnp.int32, (QUERY_GROUP, BLOCK), 0)
    column = lax.broadcasted_iota(jnp.int32, (QUERY_GROUP, BLOCK), 1)
    bit = [(n >> k) & 1 for k in range(6)]
    x_first = bit[1] * 32 + bit[2] * 16 + (n >> 4) * 4 + bit[3] * 2 + bit[0]
    y_first = bit[1] * 32 + bit[4] * 16 + ((n >> 2) & 3) * 4 + bit[5] * 2 + bit[0]
    values = events[...]
    for core, source in enumerate((x_first, y_first)):
        pick = (column == source).astype(jnp.float32)
        mine = turned(pick, values)
        for c in range(core, GROUPS, 2):
            sent[c, :QUERY_GROUP, :] = mine
    keep = mask[:1, :].astype(jnp.float32)
    scale = jnp.broadcast_to(rate[:, :1], (1, rows))
    last = jnp.concatenate([keep, scale, jnp.zeros((6, rows), jnp.float32)], axis=0)
    for c in range(GROUPS):
        sent[c, QUERY_GROUP:, :] = last


def own_queries(mask, events, rate):
    rows = events.shape[0]
    shape = (GROUPS, QUERY_GROUP + 8, rows)
    return pl.pallas_call(
        query_kernel,
        grid=(1,),
        in_specs=[
            pl.BlockSpec((8, rows), lambda i: (0, 0)),
            pl.BlockSpec((rows, BLOCK), lambda i: (0, 0)),
            pl.BlockSpec(rate.shape, lambda i: (0, 0)),
        ],
        out_specs=pl.BlockSpec(shape, lambda i: (0, 0, 0)),
        out_shape=jax.ShapeDtypeStruct(shape, jnp.float32),
        compiler_params=pltpu.CompilerParams(vmem_limit_bytes=60 << 20),
        cost_estimate=pl.CostEstimate(flops=1 << 25, bytes_accessed=1 << 19, transcendentals=0),
        name="queries",
    )(mask, events, rate)


def gram_kernel(arrived, mask, events, gram, high, low):
    rows, width = events.shape
    step = pl.program_id(0)
    blocks = width // BLOCK
    total_blocks = CHUNKS * blocks
    each = QUERIES // FAN
    squares_at = each * total_blocks
    run = QUERY_GROUP // (FAN * FAN)

    @pl.when(step == 0)
    def _():
        raw = []
        for place in range(FAN * FAN):
            parts = []
            for group in range(GROUPS):
                parts.append(arrived[group, place * run : (place + 1) * run, :])
            raw.append(jnp.concatenate(parts, axis=0))
            keeps = [
                jnp.broadcast_to(arrived[group, QUERY_GROUP : QUERY_GROUP + 1, :], (run, rows))
                for group in range(GROUPS)
            ]
            h, l = split(raw[-1] * jnp.concatenate(keeps, axis=0))
            first = place * run * GROUPS
            high[first : first + run * GROUPS, :] = h
            low[first : first + run * GROUPS, :] = l
        raw = jnp.concatenate(raw, axis=0)
        sums = turned(jnp.ones((8, rows), jnp.float32), raw * raw)[:1]
        last = jnp.concatenate([sums[:, k : k + BLOCK] for k in range(0, QUERIES, BLOCK)], axis=0)
        pad = EXTRA - total_blocks - QUERIES // BLOCK
        last = jnp.concatenate([last, jnp.zeros((pad, BLOCK), jnp.float32)], axis=0)
        for place in range(FAN):
            gram[place, squares_at + total_blocks :, :] = last

    values = events[...]
    squares = jnp.sum(values * values, axis=0, keepdims=True)
    for b in range(blocks):
        for place in range(FAN):
            gram[place, pl.ds(squares_at + step * blocks + b, 1), :] = squares[
                :, b * BLOCK : (b + 1) * BLOCK
            ]
    keep = mask[...].astype(jnp.float32)
    keep = jnp.concatenate([keep, jnp.zeros((BLOCK - blocks, rows), jnp.float32)], axis=0).T
    query_high, query_low = high[...], low[...]
    pair = 2 * BLOCK
    for start in range(0, width, pair):
        parts = []
        for at in range(start, start + pair, BLOCK):
            b = at // BLOCK
            parts.append(values[:, at : at + BLOCK] * keep[:, b : b + 1])
        h, l = split(jnp.concatenate(parts, axis=1))
        dot = functools.partial(jnp.dot, preferred_element_type=jnp.float32)
        result = dot(query_high, h) + (dot(query_high, l) + dot(query_low, h))
        for place in range(FAN):
            for at in range(0, pair, BLOCK):
                block = step * blocks + (start + at) // BLOCK
                gram[place, pl.ds(block, each, stride=total_blocks), :] = result[
                    place * each : (place + 1) * each, at : at + BLOCK
                ]


def local_gram(arrived, mask, events):
    rows, columns = events.shape
    width = columns // CHUNKS
    shape = (FAN, QUERIES // FAN * (columns // BLOCK) + EXTRA, BLOCK)
    return pl.pallas_call(
        gram_kernel,
        grid=(CHUNKS,),
        in_specs=[
            pl.BlockSpec(arrived.shape, lambda i: (0, 0, 0)),
            pl.BlockSpec((width // BLOCK, rows), lambda i: (i, 0)),
            pl.BlockSpec((rows, width), lambda i: (0, i)),
        ],
        out_specs=pl.BlockSpec(shape, lambda i: (0, 0, 0)),
        out_shape=jax.ShapeDtypeStruct(shape, jnp.float32),
        scratch_shapes=[pltpu.VMEM((QUERIES, rows), jnp.bfloat16)] * 2,
        compiler_params=pltpu.CompilerParams(
            dimension_semantics=("arbitrary",), vmem_limit_bytes=60 << 20
        ),
        cost_estimate=pl.CostEstimate(
            flops=6 * QUERIES * rows * columns,
            bytes_accessed=4 * (rows * columns + QUERIES * columns),
            transcendentals=0,
        ),
        name="gram",
    )(arrived, mask, events)


def exchanged(parts, groups):
    return lax.all_to_all(
        parts, ALL, split_axis=0, concat_axis=0, tiled=True, axis_index_groups=groups
    )


def parted(value, count):
    main, extra = value[:-EXTRA], value[-EXTRA:]
    main = main.reshape(count, -1, BLOCK)
    extra = jnp.broadcast_to(extra, (count, *extra.shape))
    return jnp.concatenate([main, extra], axis=1)


def shards(events, sample_mask, keep_rate):
    rows, columns = events.shape
    first, second, third = stages()
    share = QUERIES // (FAN * FAN * FAR)
    mask = sample_mask.T

    sent = own_queries(mask, events, keep_rate[None])
    arrived = lax.all_to_all(sent, "cols", split_axis=0, concat_axis=0, tiled=True)
    query_rate = arrived[:, QUERY_GROUP + 1, 0]

    total = exchanged(local_gram(arrived, mask, events), first).sum(axis=0)
    total = exchanged(parted(total, FAN), second).sum(axis=0)
    total = exchanged(parted(total, FAR), third).sum(axis=0)
    gram = total[:-EXTRA].reshape(share, columns)
    blocks = columns // BLOCK
    column_squares = total[-EXTRA : blocks - EXTRA].reshape(1, columns)
    query_squares = total[blocks - EXTRA : blocks - EXTRA + QUERIES // BLOCK].reshape(QUERIES)

    z, x, y, c = (lax.axis_index(a) for a in ALL)
    pairs = y * 2 + z % 2
    place = jnp.where(c % 2 == 0, x * FAN + pairs, pairs * FAN + x)
    owned = lax.dynamic_slice_in_dim(query_squares, place * (FAR * share) + z // 2 * share, share)
    owner_rate = lax.dynamic_slice_in_dim(query_rate, z // (DEPTH // GROUPS), 1)
    query_weight = lax.rsqrt(owned * owner_rate + EPSILON)
    rates = jnp.broadcast_to(keep_rate[:, None], (blocks, BLOCK)).reshape(1, columns)
    column_weight = lax.rsqrt(column_squares * rates + EPSILON)
    factor = math.sqrt(rows * DEPTH * WIDTH * PAIR)
    return factor * query_weight[:, None] * gram * column_weight


def solution(mesh):
    torus = Mesh(mesh.devices.reshape(DEPTH, WIDTH, PAIR, GROUPS), ALL)
    return jax.shard_map(
        shards,
        mesh=torus,
        in_specs=(P(ROWS, "cols"), P(ROWS, "cols"), P("cols")),
        out_specs=P(ROWS, "cols"),
        check_vma=False,
    )
```

time: 175 us -> 118 us (0.67)
  waiting for transfers between devices: 81.7 us -> 25.2 us
  blocking collectives: 11.3 us -> 63.5 us
  starting transfers between devices: 61.5 us -> 10.4 us
  local copies, waits for them, and re-layouts: 7.65 us -> 1.38 us
  Pallas kernels: 6.13 us -> 11.5 us
    ppermute x7 -> x0, waiting for transfers between devices: 61.1 us -> none  [summed_by_pairs(): lax.ppermute(value, axis, [(i, i ^ apart) for i in range(size)])]
    all_to_all x1 -> x3, blocking collectives: 11.3 us -> 63.5 us  [the longest x2 51.4 us: exchanged(): lax.all_to_all(parts, ALL, split_axis=0, concat_axis=0, tiled=True, axis_...]
    ppermute x7 -> x0, starting transfers between devices: 40.6 us -> none  [summed_by_pairs(): lax.ppermute(value, axis, [(i, i ^ apart) for i in range(size)])]
    all_to_all x2 -> x1, starting transfers between devices: 21 us -> 10.4 us  [exchanged(): lax.all_to_all(parts, ALL, split_axis=0, concat_axis=0, tiled=True, axis_...]
    unnamed x9 -> x2, local copies, waits for them, and re-layouts: 4.95 us -> 0.01 us
    all_to_all x2 -> x1, waiting for transfers between devices: 20.6 us -> 25.2 us  [exchanged(): lax.all_to_all(parts, ALL, split_axis=0, concat_axis=0, tiled=True, axis_...]
    pallas_call x1, Pallas kernels: 6.13 us -> 9.45 us  [local_gram(): pl.pallas_call(gram_kernel, grid=(CHUNKS,), in_specs=[pl.BlockSpec(arrive...]
    pallas_call x0 -> x1, Pallas kernels: none -> 2.01 us  [own_queries(): pl.pallas_call(query_kernel, grid=(1,), in_specs=[pl.BlockSpec((8, rows),...]
  transfers between devices with their start and end apart: 9 -> 1, of which waited for: 8 -> 1; matrix products, arithmetic and copies ran while one was open for 1% -> 1% of each run, Pallas kernels for 0% -> 0%
where the time goes in v2:
time: 118 us; the launch traced here: 117 us
  blocking collectives  63.5 us (54%)
  waiting for transfers between devices  25.2 us (21%)
  Pallas kernels  11.5 us (10%)
  starting transfers between devices  10.4 us (9%)
  other arithmetic  5.02 us (4%)
  local copies, waits for them, and re-layouts  1.38 us (1%)
    all_to_all x2, blocking collectives, exchanged(): lax.all_to_all(parts, ALL, split_axis=0, concat_axis=0, tiled=True, axis_...  51.4 us
    all_to_all x1, waiting for transfers between devices, exchanged(): lax.all_to_all(parts, ALL, split_axis=0, concat_axis=0, tiled=True, axis_...  25.2 us
    all_to_all x1, blocking collectives, shards(): lax.all_to_all(sent, 'cols', split_axis=0, concat_axis=0, tiled=True)  12 us
    all_to_all x1, starting transfers between devices, exchanged(): lax.all_to_all(parts, ALL, split_axis=0, concat_axis=0, tiled=True, axis_...  10.4 us
    pallas_call x1, Pallas kernels, local_gram(): pl.pallas_call(gram_kernel, grid=(CHUNKS,), in_specs=[pl.BlockSpec(arrive...  9.45 us
    reduce_sum x1, other arithmetic, shards(): total = exchanged(local_gram(arrived, mask, events), first).sum(axis=0)  2.55 us
  transfers between devices with their start and end apart: 1, of which 1 were waited for; matrix products, arithmetic and copies ran while one was open for 1% of the time, Pallas kernels for 0%

profile of v2, /device:TPU:8, one launch (start us, length us, event | category | flops | bytes accessed | tf_op | source)
XLA Modules:
  0.0 117.0 jit_solution(4637189268974965408)
XLA Ops:
  0.0 2.0 %queries.1 = f32[4,72,256]{2,1,0:T(8,128)} custom-call(s32[32,256]{1,0:T(8,128)} %bitcast.11, f32[256,4096]{1,0:T(8,128)} %events.3, f32[1,32]{1,0:T(1,128)} %bitcast.13), custom_call_target="tpu_custom_call" | custom-call | flops 33554432 | bytes 524288 | tf_op jit(solution)/shard_map/queries/pallas_call | solution.py:104
  2.0 12.0 %all_to_all.20.arrived = f32[4,72,256]{2,1,0:T(8,128)} all-to-all(f32[4,72,256]{2,1,0:T(8,128)} %queries.1), channel_id=1, replica_groups=mesh['z'=16,'x'=4,'y'=2,'cols'=4] {'cols'}, dimensions={0} | all-to-all | bytes 589824 | tf_op jit(solution)/shard_map/all_to_all | solution.py:227
  14.1 9.5 %gram.1 = f32[4,2088,128]{2,1,0:T(8,128)} custom-call(f32[4,72,256]{2,1,0:T(8,128)} %all_to_all.20.arrived, s32[32,256]{1,0:T(8,128)} %bitcast.12, f32[256,4096]{1,0:T(8,128)} %events.3), custom_call_target="tpu_custom_call" | custom-call | flops 1610612736 | bytes 8388608 | tf_op jit(solution)/shard_map/gram/pallas_call | solution.py:184
  23.5 33.9 %all_to_all.21 = f32[4,2088,128]{2,1,0:T(8,128)} all-to-all(f32[4,2088,128]{2,1,0:T(8,128)} %gram.1), channel_id=1, replica_groups={{0,8,16,24},{4,12,20,28},{32,40,48,56},{36,44,52,60},{64,72,80,88},{68,..., dimensions={0} | all-to-all | bytes 8552448 | tf_op jit(solution)/shard_map/all_to_all | solution.py:208
  57.4 2.6 %reduce_sum.27 = f32[2088,128]{1,0:T(8,128)S(1)} reduce(f32[4,2088,128]{2,1,0:T(8,128)} %all_to_all.21, f32[]{:T(128)} %constant.54.clone.1), dimensions={0}, to_apply=%region_0.0 | reduce | flops 801792 | bytes 5345284 | tf_op jit(solution)/shard_map/reduce_sum | solution.py:230
  60.0 0.1 slice.32
  60.1 0.1 pad_maximum_fusion
  60.2 17.5 %all_to_all.22 = f32[4,552,128]{2,1,0:T(8,128)S(1)} all-to-all(f32[4,552,128]{2,1,0:T(8,128)S(1)} %pad_maximum_fusion), channel_id=1, replica_groups={{0,32,4,36},{8,40,12,44},{16,48,20,52},{24,56,28,60},{64,96,68,100},{72..., dimensions={0} | all-to-all | bytes 2260992 | tf_op jit(solution)/shard_map/all_to_all | solution.py:208
  77.7 0.1 reduce_sum.28
  77.8 0.0 copy-start
  77.8 0.8 pad_maximum_fusion.1
  78.6 10.4 %all-to-all-start.3 = ((f32[8,104,128]{2,1,0:T(8,128)}), f32[8,104,128]{2,1,0:T(8,128)S(1)}, u32[]{:S(2)}, u32[]{:S(2)}) async-start(f32[8,104,128]{2,1,0:T(8,128)} %pad_maximum_fusion.1), calls=%async_computation.3 | async-start | bytes 851968 | tf_op jit(solution)/shard_map/all_to_all | solution.py:208
  89.0 0.7 slice.37
  89.7 0.5 constant_dynamic-slice_fusion
  90.2 25.2 %all-to-all-done.3 = f32[8,104,128]{2,1,0:T(8,128)S(1)} async-done(((f32[8,104,128]{2,1,0:T(8,128)}), f32[8,104,128]{2,1,0:T(8,128)S(1)}, u32[]{:S(2)}, u32[]{:S(2)}) %all-to-all-start.3) | async-done | bytes 426016 | tf_op jit(solution)/shard_map/all_to_all | solution.py:208
  115.5 0.0 copy-done
  115.5 0.1 fusion.2
  115.6 0.7 rsqrt_multiply_fusion
  116.3 0.7 multiply_multiply_fusion
  (9 shorter events, 0.1 us)
Async XLA Ops:
  77.8 37.6 %copy-start = (f32[32]{0:T(128)S(1)}, f32[32]{0:T(128)}, u32[]{:S(2)}) copy-start(f32[32]{0:T(128)} %param.5) | copy-start | bytes 388
  78.6 36.8 %all-to-all-start.3 = ((f32[8,104,128]{2,1,0:T(8,128)}), f32[8,104,128]{2,1,0:T(8,128)S(1)}, u32[]{:S(2)}, u32[]{:S(2)}) async-start(f32[8,104,128]{2,1,0:T(8,128)} %pad_maximum_fusion.1), calls=%async_computation.3 | async-start | bytes 851968 | tf_op jit(solution)/shard_map/all_to_all | solution.py:208

commit v3 on v2

v3 whole, which is shorter than its diff:
```python
import functools
import math

import jax
import jax.numpy as jnp
from jax import lax
from jax.experimental import pallas as pl
from jax.experimental.pallas import tpu as pltpu
from jax.sharding import Mesh
from jax.sharding import PartitionSpec as P

QUERY_GROUP = 64
BLOCK = 128
ROWS = ("z", "x", "y")
ALL = ("z", "x", "y", "cols")
DEPTH, WIDTH, PAIR, GROUPS = 16, 4, 2, 4
FAN = 4
FAR = DEPTH // 2
QUERIES = GROUPS * QUERY_GROUP
EXTRA = 40
EPSILON = 1e-06
CHUNKS = 8


def device(z, x, y, c):
    return ((z * WIDTH + x) * PAIR + y) * GROUPS + c


def along_x():
    return {
        c: [
            [device(z, x, y, c) for x in range(WIDTH)]
            for z in range(DEPTH)
            for y in range(PAIR)
        ]
        for c in range(GROUPS)
    }


def along_pairs():
    return {
        c: [
            [device(2 * far + odd, x, y, c) for y in range(PAIR) for odd in range(2)]
            for far in range(FAR)
            for x in range(WIDTH)
        ]
        for c in range(GROUPS)
    }


def stages():
    x, pairs = along_x(), along_pairs()
    first = [g for c in range(GROUPS) for g in (pairs if c % 2 else x)[c]]
    second = [g for c in range(GROUPS) for g in (x if c % 2 else pairs)[c]]
    third = [
        [device(2 * far + odd, x, y, c) for far in range(FAR)]
        for odd in range(2)
        for x in range(WIDTH)
        for y in range(PAIR)
        for c in range(GROUPS)
    ]
    return first, second, third


def split(values):
    high = values.astype(jnp.bfloat16)
    low = (values - high.astype(jnp.float32)).astype(jnp.bfloat16)
    return high, low


def turned(left, right):
    return lax.dot_general(
        left,
        right,
        (((1,), (1,)), ((), ())),
        precision=lax.Precision.HIGHEST,
        preferred_element_type=jnp.float32,
    )


def query_kernel(mask, events, rate, sent):
    rows = events.shape[0]
    n = lax.broadcasted_iota(jnp.int32, (QUERY_GROUP, BLOCK), 0)
    column = lax.broadcasted_iota(jnp.int32, (QUERY_GROUP, BLOCK), 1)
    x, y, low, next_, query = n >> 4, (n >> 3) & 1, (n >> 2) & 1, (n >> 1) & 1, n & 1
    source = (next_ * 2 + low) * 16 + x * 4 + y * 2 + query
    sent[:QUERY_GROUP, :] = turned((column == source).astype(jnp.float32), events[...])
    keep = mask[:1, :].astype(jnp.float32)
    scale = jnp.broadcast_to(rate[:, :1], (1, rows))
    sent[QUERY_GROUP:, :] = jnp.concatenate(
        [keep, scale, jnp.zeros((6, rows), jnp.float32)], axis=0
    )


def own_queries(mask, events, rate):
    rows = events.shape[0]
    shape = (QUERY_GROUP + 8, rows)
    return pl.pallas_call(
        query_kernel,
        grid=(1,),
        in_specs=[
            pl.BlockSpec((8, rows), lambda i: (0, 0)),
            pl.BlockSpec((rows, BLOCK), lambda i: (0, 0)),
            pl.BlockSpec(rate.shape, lambda i: (0, 0)),
        ],
        out_specs=pl.BlockSpec(shape, lambda i: (0, 0)),
        out_shape=jax.ShapeDtypeStruct(shape, jnp.float32),
        compiler_params=pltpu.CompilerParams(vmem_limit_bytes=60 << 20),
        cost_estimate=pl.CostEstimate(flops=1 << 24, bytes_accessed=1 << 18, transcendentals=0),
        name="queries",
    )(mask, events, rate)


def gram_kernel(arrived, mask, events, gram, values, result, high, low, come, gone):
    rows, columns = events.shape
    width = columns // CHUNKS
    blocks = columns // BLOCK
    each = QUERIES // FAN
    extra_at = each * blocks
    run = QUERY_GROUP // (FAN * FAN)

    def incoming(k):
        part = pl.ds(k * width, width)
        return pltpu.make_async_copy(events.at[:, part], values.at[:, part], come.at[k])

    def outgoing(k):
        size = each * width // BLOCK
        part = pl.ds(k * size, size if k < CHUNKS else EXTRA)
        return pltpu.make_async_copy(result.at[:, part], gram.at[:, part], gone.at[k])

    for k in range(CHUNKS):
        incoming(k).start()

    core = lax.axis_index("cols") % 2
    raw = []
    for place in range(FAN * FAN):
        parts, keeps = [], []
        for group in range(GROUPS):
            parts.append(arrived[group, place * run : (place + 1) * run, :])
            keep = arrived[group, QUERY_GROUP : QUERY_GROUP + 1, :]
            keeps.append(jnp.broadcast_to(keep, (run, rows)))
        raw.append(jnp.concatenate(parts, axis=0))
        h, l = split(raw[-1] * jnp.concatenate(keeps, axis=0))
        at = jnp.where(core == 0, place, place % FAN * FAN + place // FAN)
        at = pl.multiple_of(at * (run * GROUPS), run * GROUPS)
        high[pl.ds(at, run * GROUPS), :] = h
        low[pl.ds(at, run * GROUPS), :] = l
    raw = jnp.concatenate(raw, axis=0)
    sums = turned(jnp.ones((8, rows), jnp.float32), raw * raw)[:1]
    last = [sums[:, k : k + BLOCK] for k in range(0, QUERIES, BLOCK)]
    last.append(jnp.zeros((EXTRA - blocks - len(last), BLOCK), jnp.float32))
    last = jnp.concatenate(last, axis=0)
    for place in range(FAN):
        result[place, extra_at + blocks :, :] = last

    keep = mask[...].astype(jnp.float32)
    keep = jnp.concatenate([keep, jnp.zeros((BLOCK - blocks, rows), jnp.float32)], axis=0).T
    query_high, query_low = high[...], low[...]
    dot = functools.partial(jnp.dot, preferred_element_type=jnp.float32)
    pair = 2 * BLOCK
    for k in range(CHUNKS):
        incoming(k).wait()
        for start in range(k * width, (k + 1) * width, pair):
            parts, squares = [], []
            for at in range(start, start + pair, BLOCK):
                b = at // BLOCK
                value = values[:, at : at + BLOCK]
                squares.append(jnp.sum(value * value, axis=0, keepdims=True))
                parts.append(value * keep[:, b : b + 1])
            h, l = split(jnp.concatenate(parts, axis=1))
            product = dot(query_high, h) + (dot(query_high, l) + dot(query_low, h))
            for place in range(FAN):
                for at in range(0, pair, BLOCK):
                    b = (start + at) // BLOCK
                    result[place, b * each : (b + 1) * each, :] = product[
                        place * each : (place + 1) * each, at : at + BLOCK
                    ]
                    result[place, extra_at + b : extra_at + b + 1, :] = squares[at // BLOCK]
        outgoing(k).start()
    outgoing(CHUNKS).start()
    for k in range(CHUNKS + 1):
        outgoing(k).wait()


def local_gram(arrived, mask, events):
    rows, columns = events.shape
    shape = (FAN, QUERIES // FAN * (columns // BLOCK) + EXTRA, BLOCK)
    whole = pl.BlockSpec(memory_space=pltpu.VMEM)
    there = pl.BlockSpec(memory_space=pl.ANY)
    return pl.pallas_call(
        gram_kernel,
        in_specs=[whole, whole, there],
        out_specs=there,
        out_shape=jax.ShapeDtypeStruct(shape, jnp.float32),
        scratch_shapes=[
            pltpu.VMEM(events.shape, jnp.float32),
            pltpu.VMEM(shape, jnp.float32),
            pltpu.VMEM((QUERIES, rows), jnp.bfloat16),
            pltpu.VMEM((QUERIES, rows), jnp.bfloat16),
            pltpu.SemaphoreType.DMA((CHUNKS,)),
            pltpu.SemaphoreType.DMA((CHUNKS + 1,)),
        ],
        compiler_params=pltpu.CompilerParams(vmem_limit_bytes=60 << 20),
        cost_estimate=pl.CostEstimate(
            flops=6 * QUERIES * rows * columns,
            bytes_accessed=4 * (rows * columns + QUERIES * columns),
            transcendentals=0,
        ),
        name="gram",
    )(arrived, mask, events)


def exchanged(parts, groups):
    return lax.all_to_all(
        parts, ALL, split_axis=0, concat_axis=0, tiled=True, axis_index_groups=groups
    )


def first_sum_kernel(arrived, total):
    rows = arrived.shape[1] - EXTRA
    each = QUERIES // FAN
    part = each // FAN

    def summed(at, size):
        whole = arrived[0, at : at + size, :]
        for sender in range(1, FAN):
            whole += arrived[sender, at : at + size, :]
        return whole

    for at in range(0, rows, each):
        whole = summed(at, each)
        for place in range(FAN):
            first = at // FAN
            total[place, first : first + part, :] = whole[place * part : (place + 1) * part]
    extra = summed(rows, EXTRA)
    for place in range(FAN):
        total[place, rows // FAN :, :] = extra


def first_sum(arrived):
    shape = (FAN, (arrived.shape[1] - EXTRA) // FAN + EXTRA, BLOCK)
    return pl.pallas_call(
        first_sum_kernel,
        out_shape=jax.ShapeDtypeStruct(shape, jnp.float32),
        compiler_params=pltpu.CompilerParams(vmem_limit_bytes=32 << 20),
        cost_estimate=pl.CostEstimate(
            flops=arrived.size, bytes_accessed=5 * arrived.size, transcendentals=0
        ),
        name="first_sum",
    )(arrived)


def second_sum_kernel(arrived, total, whole):
    rows = arrived.shape[1] - EXTRA
    value = arrived[0]
    for sender in range(1, FAN):
        value += arrived[sender]
    whole[...] = value
    each = QUERIES // (FAN * FAN)
    share = each // FAR
    blocks = rows // each
    for place in range(FAR):
        for query in range(share):
            total[place, query * blocks : (query + 1) * blocks, :] = whole[
                pl.ds(place * share + query, blocks, stride=each), :
            ]
        total[place, share * blocks :, :] = value[rows:]


def second_sum(arrived):
    shape = (FAR, (arrived.shape[1] - EXTRA) // FAR + EXTRA, BLOCK)
    return pl.pallas_call(
        second_sum_kernel,
        out_shape=jax.ShapeDtypeStruct(shape, jnp.float32),
        scratch_shapes=[pltpu.VMEM(arrived.shape[1:], jnp.float32)],
        compiler_params=pltpu.CompilerParams(vmem_limit_bytes=32 << 20),
        cost_estimate=pl.CostEstimate(
            flops=arrived.size, bytes_accessed=5 * arrived.size, transcendentals=0
        ),
        name="second_sum",
    )(arrived)


def last_sum_kernel(factor, arrived, queries, rates, similarity):
    total = arrived[0]
    for sender in range(1, FAR):
        total += arrived[sender]
    share, columns = similarity.shape
    blocks = columns // BLOCK
    squares = total[share * blocks : (share + 1) * blocks]
    weight = lax.rsqrt(squares * rates[...] + EPSILON) * factor

    z, x, y = (lax.axis_index(a) for a in ROWS)
    mine = ((x * FAN + y * 2 + z % 2) * FAR + z // 2) * share
    group = z // (DEPTH // GROUPS)
    query_squares = total[(share + 1) * blocks : (share + 1) * blocks + QUERIES // BLOCK]
    row = lax.broadcasted_iota(jnp.int32, query_squares.shape, 0)
    lane = lax.broadcasted_iota(jnp.int32, query_squares.shape, 1)
    query_rate = queries[0, 1:2, :1]
    for k in range(1, GROUPS):
        query_rate = jnp.where(group == k, queries[k, 1:2, :1], query_rate)
    for query in range(share):
        found = jnp.where(row * BLOCK + lane == mine + query, query_squares, 0.0)
        found = jnp.sum(jnp.sum(found, axis=1, keepdims=True), axis=0, keepdims=True)
        scale = lax.rsqrt(found * query_rate + EPSILON)
        result = total[query * blocks : (query + 1) * blocks] * weight * scale
        for b in range(blocks):
            similarity[query : query + 1, b * BLOCK : (b + 1) * BLOCK] = result[b : b + 1]


def last_sum(factor, arrived, queries, rates):
    blocks, share = rates.shape[0], QUERIES // (FAN * FAN * FAR)
    shape = (share, blocks * BLOCK)
    whole = lambda a: pl.BlockSpec(a.shape, lambda i: (0,) * a.ndim)
    return pl.pallas_call(
        functools.partial(last_sum_kernel, factor),
        grid=(1,),
        in_specs=[
            whole(arrived),
            pl.BlockSpec((GROUPS, 8, queries.shape[2]), lambda i: (0, QUERY_GROUP // 8, 0)),
            whole(rates),
        ],
        out_specs=pl.BlockSpec(shape, lambda i: (0, 0)),
        out_shape=jax.ShapeDtypeStruct(shape, jnp.float32),
        compiler_params=pltpu.CompilerParams(vmem_limit_bytes=32 << 20),
        cost_estimate=pl.CostEstimate(
            flops=arrived.size, bytes_accessed=5 * arrived.size, transcendentals=0
        ),
        name="last_sum",
    )(arrived, queries, rates)


def shards(events, sample_mask, keep_rate):
    first, second, third = stages()
    mask = sample_mask.T
    arrived = lax.all_gather(own_queries(mask, events, keep_rate[None]), "cols")
    total = first_sum(exchanged(local_gram(arrived, mask, events), first))
    total = second_sum(exchanged(total, second))
    factor = math.sqrt(events.shape[0] * DEPTH * WIDTH * PAIR)
    rates = jnp.broadcast_to(keep_rate[:, None], (keep_rate.size, BLOCK))
    return last_sum(factor, exchanged(total, third), arrived, rates)


def solution(mesh):
    torus = Mesh(mesh.devices.reshape(DEPTH, WIDTH, PAIR, GROUPS), ALL)
    return jax.shard_map(
        shards,
        mesh=torus,
        in_specs=(P(ROWS, "cols"), P(ROWS, "cols"), P("cols")),
        out_specs=P(ROWS, "cols"),
        check_vma=False,
    )
```

time: 118 us -> 107 us (0.907)
  the two profiles are of different devices: /device:TPU:8 before, /device:TPU:2 now
where the time goes in v3:
time: 107 us
  blocking collectives  96 us (90%)
  Pallas kernels  11 us (10%)
    all_to_all x3, blocking collectives, exchanged(): lax.all_to_all(parts, ALL, split_axis=0, concat_axis=0, tiled=True, axis_...  86.8 us
    all_gather x1, blocking collectives, shards(): arrived = lax.all_gather(own_queries(mask, events, keep_rate[None]), 'cols')  9.18 us
    pallas_call x1, Pallas kernels, local_gram(): pl.pallas_call(gram_kernel, in_specs=[whole, whole, there], out_specs=the...  8.05 us

profile of v3, /device:TPU:2, one launch (start us, length us, event | category | flops | bytes accessed | tf_op | source)
XLA Modules:
  0.0 107.1 jit_solution(3229096623993902484)
XLA Ops:
  0.0 1.8 %queries.1 = f32[72,256]{1,0:T(8,128)} custom-call(s32[32,256]{1,0:T(8,128)} %bitcast.5, f32[256,4096]{1,0:T(8,128)} %events.3, f32[1,32]{1,0:T(1,128)} %bitcast.7), custom_call_target="tpu_custom_call" | custom-call | flops 16777216 | bytes 262144 | tf_op jit(solution)/shard_map/queries/pallas_call | solution.py:98
  1.8 9.2 %all-gather = f32[288,256]{1,0:T(8,128)} all-gather(f32[72,256]{1,0:T(8,128)} %queries.1), channel_id=2, replica_groups=mesh['z'=16,'x'=4,'y'=2,'cols'=4] {'cols'}, dimensions={0}, use_global_device_ids=true | all-gather | bytes 368640 | tf_op jit(solution)/shard_map/all_gather | solution.py:336
  10.9 8.1 %gram.1 = f32[4,2088,128]{2,1,0:T(8,128)} custom-call(f32[4,72,256]{2,1,0:T(8,128)} %bitcast.3, s32[32,256]{1,0:T(8,128)} %bitcast.6, f32[256,4096]{1,0:T(8,128)} %events.3), custom_call_target="tpu_custom_call" | custom-call | flops 1610612736 | bytes 8388608 | tf_op jit(solution)/shard_map/gram/pallas_call | solution.py:190
  19.0 35.3 %all_to_all.15.arrived = f32[4,2088,128]{2,1,0:T(8,128)S(1)} all-to-all(f32[4,2088,128]{2,1,0:T(8,128)} %gram.1), channel_id=1, replica_groups={{0,8,16,24},{4,12,20,28},{32,40,48,56},{36,44,52,60},{64,72,80,88},{68,..., dimensions={0} | all-to-all | bytes 8552448 | tf_op jit(solution)/shard_map/all_to_all | solution.py:214
  54.3 0.0 copy-start.1
  54.3 0.0 copy-start
  54.3 0.2 first_sum.1
  54.5 12.9 %all_to_all.16.arrived = f32[4,552,128]{2,1,0:T(8,128)S(1)} all-to-all(f32[4,552,128]{2,1,0:T(8,128)S(1)} %first_sum.1), channel_id=1, replica_groups={{0,32,4,36},{8,40,12,44},{16,48,20,52},{24,56,28,60},{64,96,68,100},{72..., dimensions={0} | all-to-all | bytes 2260992 | tf_op jit(solution)/shard_map/all_to_all | solution.py:214
  67.4 0.2 second_sum.1
  67.5 38.7 %all_to_all.17.arrived = f32[8,104,128]{2,1,0:T(8,128)S(1)} all-to-all(f32[8,104,128]{2,1,0:T(8,128)S(1)} %second_sum.1), channel_id=1, replica_groups={{0,64,128,192,256,320,384,448},{1,65,129,193,257,321,385,449},{2,66,130..., dimensions={0} | all-to-all | bytes 851968 | tf_op jit(solution)/shard_map/all_to_all | solution.py:214
  106.2 0.0 copy-done.1
  106.2 0.1 broadcast_in_dim.10.rates
  106.3 0.0 copy-done
  106.3 0.8 last_sum.1
Async XLA Ops:
  54.3 51.9 %copy-start.1 = (f32[32]{0:T(128)S(1)}, f32[32]{0:T(128)}, u32[]{:S(2)}) copy-start(f32[32]{0:T(128)} %param.5) | copy-start | bytes 388
  54.3 52.0 %copy-start = (f32[288,256]{1,0:T(8,128)S(1)}, f32[288,256]{1,0:T(8,128)}, u32[]{:S(2)}) copy-start(f32[288,256]{1,0:T(8,128)} %all-gather) | copy-start | bytes 884740

commit v4 on v3

--- a/solution.py
+++ b/solution.py
@@ -19,7 +19,6 @@
 QUERIES = GROUPS * QUERY_GROUP
 EXTRA = 40
 EPSILON = 1e-06
-CHUNKS = 8
 
 
 def device(z, x, y, c):
@@ -78,18 +77,21 @@
     )
 
 
-def query_kernel(mask, events, rate, sent):
-    rows = events.shape[0]
+def query_kernel(mask, near, rate, events, sent, held, come):
+    incoming = pltpu.make_async_copy(events, held, come)
+    incoming.start()
+    rows = near.shape[0]
     n = lax.broadcasted_iota(jnp.int32, (QUERY_GROUP, BLOCK), 0)
     column = lax.broadcasted_iota(jnp.int32, (QUERY_GROUP, BLOCK), 1)
     x, y, low, next_, query = n >> 4, (n >> 3) & 1, (n >> 2) & 1, (n >> 1) & 1, n & 1
     source = (next_ * 2 + low) * 16 + x * 4 + y * 2 + query
-    sent[:QUERY_GROUP, :] = turned((column == source).astype(jnp.float32), events[...])
+    sent[:QUERY_GROUP, :] = turned((column == source).astype(jnp.float32), near[...])
     keep = mask[:1, :].astype(jnp.float32)
     scale = jnp.broadcast_to(rate[:, :1], (1, rows))
     sent[QUERY_GROUP:, :] = jnp.concatenate(
         [keep, scale, jnp.zeros((6, rows), jnp.float32)], axis=0
     )
+    incoming.wait()
 
 
 def own_queries(mask, events, rate):
@@ -102,34 +104,29 @@
             pl.BlockSpec((8, rows), lambda i: (0, 0)),
             pl.BlockSpec((rows, BLOCK), lambda i: (0, 0)),
             pl.BlockSpec(rate.shape, lambda i: (0, 0)),
-        ],
-        out_specs=pl.BlockSpec(shape, lambda i: (0, 0)),
-        out_shape=jax.ShapeDtypeStruct(shape, jnp.float32),
-        compiler_params=pltpu.CompilerParams(vmem_limit_bytes=60 << 20),
-        cost_estimate=pl.CostEstimate(flops=1 << 24, bytes_accessed=1 << 18, transcendentals=0),
+            pl.BlockSpec(memory_space=pl.ANY),
+        ],
+        out_specs=[
+            pl.BlockSpec(shape, lambda i: (0, 0)),
+            pl.BlockSpec(memory_space=pltpu.VMEM),
+        ],
+        out_shape=[
+            jax.ShapeDtypeStruct(shape, jnp.float32),
+            jax.ShapeDtypeStruct(events.shape, jnp.float32),
+        ],
+        scratch_shapes=[pltpu.SemaphoreType.DMA],
+        compiler_params=pltpu.CompilerParams(vmem_limit_bytes=46 << 20),
+        cost_estimate=pl.CostEstimate(flops=1 << 24, bytes_accessed=1 << 23, transcendentals=0),
         name="queries",
-    )(mask, events, rate)
-
-
-def gram_kernel(arrived, mask, events, gram, values, result, high, low, come, gone):
-    rows, columns = events.shape
-    width = columns // CHUNKS
+    )(mask, events, rate, events)
+
+
+def gram_kernel(arrived, mask, values, result, high, low):
+    rows, columns = values.shape
     blocks = columns // BLOCK
     each = QUERIES // FAN
     extra_at = each * blocks
     run = QUERY_GROUP // (FAN * FAN)
-
-    def incoming(k):
-        part = pl.ds(k * width, width)
-        return pltpu.make_async_copy(events.at[:, part], values.at[:, part], come.at[k])
-
-    def outgoing(k):
-        size = each * width // BLOCK
-        part = pl.ds(k * size, size if k < CHUNKS else EXTRA)
-        return pltpu.make_async_copy(result.at[:, part], gram.at[:, part], gone.at[k])
-
-    for k in range(CHUNKS):
-        incoming(k).start()
 
     core = lax.axis_index("cols") % 2
     raw = []
@@ -156,51 +153,42 @@
     keep = mask[...].astype(jnp.float32)
     keep = jnp.concatenate([keep, jnp.zeros((BLOCK - blocks, rows), jnp.float32)], axis=0).T
     query_high, query_low = high[...], low[...]
+    query_all = jnp.concatenate([query_high, query_high, query_low], axis=1)
     dot = functools.partial(jnp.dot, preferred_element_type=jnp.float32)
     pair = 2 * BLOCK
-    for k in range(CHUNKS):
-        incoming(k).wait()
-        for start in range(k * width, (k + 1) * width, pair):
-            parts, squares = [], []
-            for at in range(start, start + pair, BLOCK):
-                b = at // BLOCK
-                value = values[:, at : at + BLOCK]
-                squares.append(jnp.sum(value * value, axis=0, keepdims=True))
-                parts.append(value * keep[:, b : b + 1])
-            h, l = split(jnp.concatenate(parts, axis=1))
-            product = dot(query_high, h) + (dot(query_high, l) + dot(query_low, h))
+    for start in range(0, columns, pair):
+        parts = []
+        for at in range(start, start + pair, BLOCK):
+            b = at // BLOCK
+            value = values[:, at : at + BLOCK]
+            square = jnp.sum(value * value, axis=0, keepdims=True)
             for place in range(FAN):
-                for at in range(0, pair, BLOCK):
-                    b = (start + at) // BLOCK
-                    result[place, b * each : (b + 1) * each, :] = product[
-                        place * each : (place + 1) * each, at : at + BLOCK
-                    ]
-                    result[place, extra_at + b : extra_at + b + 1, :] = squares[at // BLOCK]
-        outgoing(k).start()
-    outgoing(CHUNKS).start()
-    for k in range(CHUNKS + 1):
-        outgoing(k).wait()
+                result[place, extra_at + b : extra_at + b + 1, :] = square
+            parts.append(value * keep[:, b : b + 1])
+        h, l = split(jnp.concatenate(parts, axis=1))
+        product = dot(query_all, jnp.concatenate([h, l, h], axis=0))
+        for place in range(FAN):
+            for at in range(0, pair, BLOCK):
+                b = (start + at) // BLOCK
+                result[place, b * each : (b + 1) * each, :] = product[
+                    place * each : (place + 1) * each, at : at + BLOCK
+                ]
 
 
 def local_gram(arrived, mask, events):
     rows, columns = events.shape
     shape = (FAN, QUERIES // FAN * (columns // BLOCK) + EXTRA, BLOCK)
     whole = pl.BlockSpec(memory_space=pltpu.VMEM)
-    there = pl.BlockSpec(memory_space=pl.ANY)
     return pl.pallas_call(
         gram_kernel,
-        in_specs=[whole, whole, there],
-        out_specs=there,
+        in_specs=[whole, whole, whole],
+        out_specs=whole,
         out_shape=jax.ShapeDtypeStruct(shape, jnp.float32),
         scratch_shapes=[
-            pltpu.VMEM(events.shape, jnp.float32),
-            pltpu.VMEM(shape, jnp.float32),
             pltpu.VMEM((QUERIES, rows), jnp.bfloat16),
             pltpu.VMEM((QUERIES, rows), jnp.bfloat16),
-            pltpu.SemaphoreType.DMA((CHUNKS,)),
-            pltpu.SemaphoreType.DMA((CHUNKS + 1,)),
-        ],
-        compiler_params=pltpu.CompilerParams(vmem_limit_bytes=60 << 20),
+        ],
+        compiler_params=pltpu.CompilerParams(vmem_limit_bytes=32 << 20),
         cost_estimate=pl.CostEstimate(
             flops=6 * QUERIES * rows * columns,
             bytes_accessed=4 * (rows * columns + QUERIES * columns),
@@ -333,7 +321,8 @@
 def shards(events, sample_mask, keep_rate):
     first, second, third = stages()
     mask = sample_mask.T
-    arrived = lax.all_gather(own_queries(mask, events, keep_rate[None]), "cols")
+    own, events = own_queries(mask, events, keep_rate[None])
+    arrived = lax.all_gather(own, "cols")
     total = first_sum(exchanged(local_gram(arrived, mask, events), first))
     total = second_sum(exchanged(total, second))
     factor = math.sqrt(events.shape[0] * DEPTH * WIDTH * PAIR)

time: 107 us -> 103 us (0.963)
  the two profiles are of different devices: /device:TPU:2 before, /device:TPU:16 now
where the time goes in v4:
time: 103 us; the launch traced here: 102 us
  blocking collectives  94.1 us (91%)
  Pallas kernels  6.69 us (6%)
  local copies, waits for them, and re-layouts  1.48 us (1%)
    all_to_all x3, blocking collectives, exchanged(): lax.all_to_all(parts, ALL, split_axis=0, concat_axis=0, tiled=True, axis_...  84 us
    all_gather x1, blocking collectives, shards(): arrived = lax.all_gather(own, 'cols')  10.1 us
    pallas_call x1, Pallas kernels, own_queries(): pl.pallas_call(query_kernel, grid=(1,), in_specs=[pl.BlockSpec((8, rows),...  3.1 us
    pallas_call x1, Pallas kernels, local_gram(): pl.pallas_call(gram_kernel, in_specs=[whole, whole, whole], out_specs=who...  2.44 us

profile of v4, /device:TPU:16, one launch (start us, length us, event | category | flops | bytes accessed | tf_op | source)
XLA Modules:
  0.0 102.3 jit_solution(14540587926045273467)
XLA Ops:
  0.0 0.0 copy-start
  0.0 0.8 copy-done
  0.8 0.0 copy-start.1
  0.8 0.7 copy-done.1
  1.4 3.1 %queries.1 = (f32[72,256]{1,0:T(8,128)S(1)}, f32[256,4096]{1,0:T(8,128)S(1)}) custom-call(s32[32,256]{1,0:T(8,128)S(1)} %bitcast.5, f32[256,4096]{1,0:T(8,128)} %events.1, f32[1,32]{1,0:T(1,128)S(1)} %bitcast.7, f32[256,4096]{1,0:T(8,128)} %events.1), custom_call_target="tpu_custom_call" | custom-call | flops 16777216 | bytes 8388608 | tf_op jit(solution)/shard_map/queries/pallas_call | solution.py:100
  4.5 10.1 %all-gather = f32[288,256]{1,0:T(8,128)S(1)} all-gather(f32[72,256]{1,0:T(8,128)S(1)} %get-tuple-element.7), channel_id=2, replica_groups=mesh['z'=16,'x'=4,'y'=2,'cols'=4] {'cols'}, dimensions={0}, use_global_device_ids=true | all-gather | bytes 368640 | tf_op jit(solution)/shard_map/all_gather | solution.py:325
  14.7 2.4 %gram.1 = f32[4,2088,128]{2,1,0:T(8,128)S(1)} custom-call(f32[4,72,256]{2,1,0:T(8,128)S(1)} %bitcast.3, s32[32,256]{1,0:T(8,128)S(1)} %bitcast.6, f32[256,4096]{1,0:T(8,128)S(1)} %get-tuple-element.8.values), custom_call_target="tpu_custom_call" | custom-call | flops 1610612736 | bytes 8388608 | tf_op jit(solution)/shard_map/gram/pallas_call | solution.py:182
  17.1 30.7 %all_to_all.15.arrived = f32[4,2088,128]{2,1,0:T(8,128)S(1)} all-to-all(f32[4,2088,128]{2,1,0:T(8,128)S(1)} %gram.1), channel_id=1, replica_groups={{0,8,16,24},{4,12,20,28},{32,40,48,56},{36,44,52,60},{64,72,80,88},{68,..., dimensions={0} | all-to-all | bytes 8552448 | tf_op jit(solution)/shard_map/all_to_all | solution.py:202
  47.9 0.2 first_sum.1
  48.0 13.0 %all_to_all.16.arrived = f32[4,552,128]{2,1,0:T(8,128)S(1)} all-to-all(f32[4,552,128]{2,1,0:T(8,128)S(1)} %first_sum.1), channel_id=1, replica_groups={{0,32,4,36},{8,40,12,44},{16,48,20,52},{24,56,28,60},{64,96,68,100},{72..., dimensions={0} | all-to-all | bytes 2260992 | tf_op jit(solution)/shard_map/all_to_all | solution.py:202
  61.0 0.2 second_sum.1
  61.2 40.3 %all_to_all.17.arrived = f32[8,104,128]{2,1,0:T(8,128)S(1)} all-to-all(f32[8,104,128]{2,1,0:T(8,128)S(1)} %second_sum.1), channel_id=1, replica_groups={{0,64,128,192,256,320,384,448},{1,65,129,193,257,321,385,449},{2,66,130..., dimensions={0} | all-to-all | bytes 851968 | tf_op jit(solution)/shard_map/all_to_all | solution.py:202
  101.5 0.1 broadcast_in_dim.10.rates
  101.5 0.8 last_sum.1
Async XLA Ops:
  0.0 0.8 copy-start
  0.8 0.7 copy-start.1

commit v5 on v4

--- a/solution.py
+++ b/solution.py
@@ -77,21 +77,18 @@
     )
 
 
-def query_kernel(mask, near, rate, events, sent, held, come):
-    incoming = pltpu.make_async_copy(events, held, come)
-    incoming.start()
-    rows = near.shape[0]
+def query_kernel(mask, events, rate, sent):
+    rows = events.shape[0]
     n = lax.broadcasted_iota(jnp.int32, (QUERY_GROUP, BLOCK), 0)
     column = lax.broadcasted_iota(jnp.int32, (QUERY_GROUP, BLOCK), 1)
     x, y, low, next_, query = n >> 4, (n >> 3) & 1, (n >> 2) & 1, (n >> 1) & 1, n & 1
     source = (next_ * 2 + low) * 16 + x * 4 + y * 2 + query
-    sent[:QUERY_GROUP, :] = turned((column == source).astype(jnp.float32), near[...])
+    sent[:QUERY_GROUP, :] = turned((column == source).astype(jnp.float32), events[...])
     keep = mask[:1, :].astype(jnp.float32)
     scale = jnp.broadcast_to(rate[:, :1], (1, rows))
     sent[QUERY_GROUP:, :] = jnp.concatenate(
         [keep, scale, jnp.zeros((6, rows), jnp.float32)], axis=0
     )
-    incoming.wait()
 
 
 def own_queries(mask, events, rate):
@@ -104,21 +101,13 @@
             pl.BlockSpec((8, rows), lambda i: (0, 0)),
             pl.BlockSpec((rows, BLOCK), lambda i: (0, 0)),
             pl.BlockSpec(rate.shape, lambda i: (0, 0)),
-            pl.BlockSpec(memory_space=pl.ANY),
         ],
-        out_specs=[
-            pl.BlockSpec(shape, lambda i: (0, 0)),
-            pl.BlockSpec(memory_space=pltpu.VMEM),
-        ],
-        out_shape=[
-            jax.ShapeDtypeStruct(shape, jnp.float32),
-            jax.ShapeDtypeStruct(events.shape, jnp.float32),
-        ],
-        scratch_shapes=[pltpu.SemaphoreType.DMA],
-        compiler_params=pltpu.CompilerParams(vmem_limit_bytes=46 << 20),
-        cost_estimate=pl.CostEstimate(flops=1 << 24, bytes_accessed=1 << 23, transcendentals=0),
+        out_specs=pl.BlockSpec(shape, lambda i: (0, 0)),
+        out_shape=jax.ShapeDtypeStruct(shape, jnp.float32),
+        compiler_params=pltpu.CompilerParams(vmem_limit_bytes=56 << 20),
+        cost_estimate=pl.CostEstimate(flops=1 << 24, bytes_accessed=1 << 18, transcendentals=0),
         name="queries",
-    )(mask, events, rate, events)
+    )(mask, events, rate)
 
 
 def gram_kernel(arrived, mask, values, result, high, low):
@@ -321,8 +310,7 @@
 def shards(events, sample_mask, keep_rate):
     first, second, third = stages()
     mask = sample_mask.T
-    own, events = own_queries(mask, events, keep_rate[None])
-    arrived = lax.all_gather(own, "cols")
+    arrived = lax.all_gather(own_queries(mask, events, keep_rate[None]), "cols")
     total = first_sum(exchanged(local_gram(arrived, mask, events), first))
     total = second_sum(exchanged(total, second))
     factor = math.sqrt(events.shape[0] * DEPTH * WIDTH * PAIR)

time: 103 us -> 100 us (0.971)
  local copies, waits for them, and re-layouts: 1.48 us -> 0.08 us
  Pallas kernels: 6.69 us -> 5.32 us
    unnamed x4 -> x6, local copies, waits for them, and re-layouts: 1.41 us -> 0.01 us
    pallas_call x1, Pallas kernels: 3.1 us -> 1.92 us  [own_queries(): pl.pallas_call(query_kernel, grid=(1,), in_specs=[pl.BlockSpec((8, rows),...]
where the time goes in v5:
time: 100 us; the launch traced here: 99.8 us
  blocking collectives  94.3 us (94%)
  Pallas kernels  5.32 us (5%)
    all_to_all x3, blocking collectives, exchanged(): lax.all_to_all(parts, ALL, split_axis=0, concat_axis=0, tiled=True, axis_...  84 us
    all_gather x1, blocking collectives, shards(): arrived = lax.all_gather(own_queries(mask, events, keep_rate[None]), 'cols')  10.3 us
    pallas_call x1, Pallas kernels, local_gram(): pl.pallas_call(gram_kernel, in_specs=[whole, whole, whole], out_specs=who...  2.24 us

profile of v5, /device:TPU:16, one launch (start us, length us, event | category | flops | bytes accessed | tf_op | source)
XLA Modules:
  0.0 99.8 jit_solution(16835358634507071634)
XLA Ops:
  0.0 0.0 copy-start.1
  0.0 0.0 copy-start
  0.0 1.9 %queries.1 = f32[72,256]{1,0:T(8,128)} custom-call(s32[32,256]{1,0:T(8,128)} %bitcast.5, f32[256,4096]{1,0:T(8,128)} %values.1, f32[1,32]{1,0:T(1,128)} %bitcast.7), custom_call_target="tpu_custom_call" | custom-call | flops 16777216 | bytes 262144 | tf_op jit(solution)/shard_map/queries/pallas_call | solution.py:97
  1.9 10.3 %all-gather = f32[288,256]{1,0:T(8,128)S(1)} all-gather(f32[72,256]{1,0:T(8,128)} %queries.1), channel_id=2, replica_groups=mesh['z'=16,'x'=4,'y'=2,'cols'=4] {'cols'}, dimensions={0}, use_global_device_ids=true | all-gather | bytes 368640 | tf_op jit(solution)/shard_map/all_gather | solution.py:313
  12.3 0.0 copy-done.1
  12.3 0.0 copy-done
  12.3 2.2 %gram.1 = f32[4,2088,128]{2,1,0:T(8,128)S(1)} custom-call(f32[4,72,256]{2,1,0:T(8,128)S(1)} %bitcast.3, s32[32,256]{1,0:T(8,128)S(1)} %bitcast.6, f32[256,4096]{1,0:T(8,128)S(1)} %copy-done), custom_call_target="tpu_custom_call" | custom-call | flops 1610612736 | bytes 8388608 | tf_op jit(solution)/shard_map/gram/pallas_call | solution.py:171
  14.5 30.7 %all_to_all.15.arrived = f32[4,2088,128]{2,1,0:T(8,128)S(1)} all-to-all(f32[4,2088,128]{2,1,0:T(8,128)S(1)} %gram.1), channel_id=1, replica_groups={{0,8,16,24},{4,12,20,28},{32,40,48,56},{36,44,52,60},{64,72,80,88},{68,..., dimensions={0} | all-to-all | bytes 8552448 | tf_op jit(solution)/shard_map/all_to_all | solution.py:191
  45.3 0.0 copy-start.2
  45.3 0.2 first_sum.1
  45.5 13.0 %all_to_all.16.arrived = f32[4,552,128]{2,1,0:T(8,128)S(1)} all-to-all(f32[4,552,128]{2,1,0:T(8,128)S(1)} %first_sum.1), channel_id=1, replica_groups={{0,32,4,36},{8,40,12,44},{16,48,20,52},{24,56,28,60},{64,96,68,100},{72..., dimensions={0} | all-to-all | bytes 2260992 | tf_op jit(solution)/shard_map/all_to_all | solution.py:191
  58.4 0.2 second_sum.1
  58.6 40.3 %all_to_all.17.arrived = f32[8,104,128]{2,1,0:T(8,128)S(1)} all-to-all(f32[8,104,128]{2,1,0:T(8,128)S(1)} %second_sum.1), channel_id=1, replica_groups={{0,64,128,192,256,320,384,448},{1,65,129,193,257,321,385,449},{2,66,130..., dimensions={0} | all-to-all | bytes 851968 | tf_op jit(solution)/shard_map/all_to_all | solution.py:191
  98.9 0.0 copy-done.2
  98.9 0.1 broadcast_in_dim.10.rates
  98.9 0.8 last_sum.1
Async XLA Ops:
  0.0 12.3 %copy-start.1 = (s32[256,32]{0,1:T(8,128)S(1)}, s32[256,32]{0,1:T(8,128)}, u32[]{:S(2)}) copy-start(s32[256,32]{0,1:T(8,128)} %param.4) | copy-start | bytes 98308
  0.0 12.3 %copy-start = (f32[256,4096]{1,0:T(8,128)S(1)}, f32[256,4096]{1,0:T(8,128)}, u32[]{:S(2)}) copy-start(f32[256,4096]{1,0:T(8,128)} %values.1) | copy-start | bytes 12582916
  45.3 53.6 %copy-start.2 = (f32[32]{0:T(128)S(1)}, f32[32]{0:T(128)}, u32[]{:S(2)}) copy-start(f32[32]{0:T(128)} %param.5) | copy-start | bytes 388

commit v6 on v5

--- a/solution.py
+++ b/solution.py
@@ -25,32 +25,42 @@
     return ((z * WIDTH + x) * PAIR + y) * GROUPS + c
 
 
-def along_x():
-    return {
-        c: [
-            [device(z, x, y, c) for x in range(WIDTH)]
-            for z in range(DEPTH)
-            for y in range(PAIR)
-        ]
-        for c in range(GROUPS)
-    }
-
-
-def along_pairs():
-    return {
-        c: [
-            [device(2 * far + odd, x, y, c) for y in range(PAIR) for odd in range(2)]
-            for far in range(FAR)
-            for x in range(WIDTH)
-        ]
-        for c in range(GROUPS)
-    }
+CORE_0_CLASSES = ((0, 3), (1, 2))
+CORE_1_CLASSES = ((0, 1), (3, 2))
+
+
+def block_of(core, x, y, odd):
+    if core == 0:
+        shared = next(k for k, places in enumerate(CORE_0_CLASSES) if x in places)
+        return shared * 2 + odd, CORE_0_CLASSES[shared].index(x) * 2 + y
+    shared = next(k for k, places in enumerate(CORE_1_CLASSES) if x in places)
+    return shared * 2 + y, CORE_1_CLASSES[shared].index(x) * 2 + odd
 
 
 def stages():
-    x, pairs = along_x(), along_pairs()
-    first = [g for c in range(GROUPS) for g in (pairs if c % 2 else x)[c]]
-    second = [g for c in range(GROUPS) for g in (x if c % 2 else pairs)[c]]
+    first, second = [], []
+    for c in range(0, GROUPS, 2):
+        for pair in zip(*CORE_0_CLASSES):
+            first += [
+                [device((2 * far - odd) % DEPTH, x, y, c) for x in pair for odd in range(2)]
+                for far in range(FAR)
+                for y in range(PAIR)
+            ]
+        for shared in CORE_0_CLASSES:
+            second += [
+                [device(z, x, y, c) for x in shared for y in range(PAIR)] for z in range(DEPTH)
+            ]
+    for c in range(1, GROUPS, 2):
+        for pair in zip(*CORE_1_CLASSES):
+            first += [
+                [device(z, x, y, c) for x in pair for y in range(PAIR)] for z in range(DEPTH)
+            ]
+        for shared in CORE_1_CLASSES:
+            second += [
+                [device(2 * far + odd, x, y, c) for x in shared for odd in range(2)]
+                for far in range(FAR)
+                for y in range(PAIR)
+            ]
     third = [
         [device(2 * far + odd, x, y, c) for far in range(FAR)]
         for odd in range(2)
@@ -127,7 +137,11 @@
             keeps.append(jnp.broadcast_to(keep, (run, rows)))
         raw.append(jnp.concatenate(parts, axis=0))
         h, l = split(raw[-1] * jnp.concatenate(keeps, axis=0))
-        at = jnp.where(core == 0, place, place % FAN * FAN + place // FAN)
+        spots = []
+        for each_core in range(2):
+            near, far = block_of(each_core, place // FAN, place // 2 % 2, place % 2)
+            spots.append(near * FAN + far)
+        at = jnp.where(core == 0, *spots)
         at = pl.multiple_of(at * (run * GROUPS), run * GROUPS)
         high[pl.ds(at, run * GROUPS), :] = h
         low[pl.ds(at, run * GROUPS), :] = l

time: 100 us -> 101 us (1.010)
  no operation moved by 1% of the time
where the time goes in v6:
time: 101 us; the launch traced here: 100 us
  blocking collectives  95 us (94%)
  Pallas kernels  5.31 us (5%)
    all_to_all x3, blocking collectives, exchanged(): lax.all_to_all(parts, ALL, split_axis=0, concat_axis=0, tiled=True, axis_...  84.7 us
    all_gather x1, blocking collectives, shards(): arrived = lax.all_gather(own_queries(mask, events, keep_rate[None]), 'cols')  10.3 us
    pallas_call x1, Pallas kernels, local_gram(): pl.pallas_call(gram_kernel, in_specs=[whole, whole, whole], out_specs=who...  2.24 us

profile of v6, /device:TPU:16, one launch (start us, length us, event | category | flops | bytes accessed | tf_op | source)
XLA Modules:
  0.0 100.4 jit_solution(5761537173442090849)
XLA Ops:
  0.0 0.0 copy-start.1
  0.0 0.0 copy-start
  0.0 1.9 %queries.1 = f32[72,256]{1,0:T(8,128)} custom-call(s32[32,256]{1,0:T(8,128)} %bitcast.5, f32[256,4096]{1,0:T(8,128)} %values.1, f32[1,32]{1,0:T(1,128)} %bitcast.7), custom_call_target="tpu_custom_call" | custom-call | flops 16777216 | bytes 262144 | tf_op jit(solution)/shard_map/queries/pallas_call | solution.py:107
  1.9 10.3 %all-gather = f32[288,256]{1,0:T(8,128)S(1)} all-gather(f32[72,256]{1,0:T(8,128)} %queries.1), channel_id=2, replica_groups=mesh['z'=16,'x'=4,'y'=2,'cols'=4] {'cols'}, dimensions={0}, use_global_device_ids=true | all-gather | bytes 368640 | tf_op jit(solution)/shard_map/all_gather | solution.py:327
  12.3 0.0 copy-done.1
  12.3 0.0 copy-done
  12.3 2.2 %gram.1 = f32[4,2088,128]{2,1,0:T(8,128)S(1)} custom-call(f32[4,72,256]{2,1,0:T(8,128)S(1)} %bitcast.3, s32[32,256]{1,0:T(8,128)S(1)} %bitcast.6, f32[256,4096]{1,0:T(8,128)S(1)} %copy-done), custom_call_target="tpu_custom_call" | custom-call | flops 1610612736 | bytes 8388608 | tf_op jit(solution)/shard_map/gram/pallas_call | solution.py:185
  14.5 37.4 %all_to_all.15.arrived = f32[4,2088,128]{2,1,0:T(8,128)S(1)} all-to-all(f32[4,2088,128]{2,1,0:T(8,128)S(1)} %gram.1), channel_id=1, replica_groups={{0,480,8,488},{4,484,12,492},{64,32,72,40},{68,36,76,44},{128,96,136,10..., dimensions={0} | all-to-all | bytes 8552448 | tf_op jit(solution)/shard_map/all_to_all | solution.py:205
  52.0 0.0 copy-start.2
  52.0 0.2 first_sum.1
  52.1 15.7 %all_to_all.16.arrived = f32[4,552,128]{2,1,0:T(8,128)S(1)} all-to-all(f32[4,552,128]{2,1,0:T(8,128)S(1)} %first_sum.1), channel_id=1, replica_groups={{0,4,24,28},{32,36,56,60},{64,68,88,92},{96,100,120,124},{128,132,152,1..., dimensions={0} | all-to-all | bytes 2260992 | tf_op jit(solution)/shard_map/all_to_all | solution.py:205
  67.9 0.2 second_sum.1
  68.0 31.5 %all_to_all.17.arrived = f32[8,104,128]{2,1,0:T(8,128)S(1)} all-to-all(f32[8,104,128]{2,1,0:T(8,128)S(1)} %second_sum.1), channel_id=1, replica_groups={{0,64,128,192,256,320,384,448},{1,65,129,193,257,321,385,449},{2,66,130..., dimensions={0} | all-to-all | bytes 851968 | tf_op jit(solution)/shard_map/all_to_all | solution.py:205
  99.6 0.0 copy-done.2
  99.6 0.1 broadcast_in_dim.10.rates
  99.6 0.8 last_sum.1
Async XLA Ops:
  0.0 12.3 %copy-start.1 = (s32[256,32]{0,1:T(8,128)S(1)}, s32[256,32]{0,1:T(8,128)}, u32[]{:S(2)}) copy-start(s32[256,32]{0,1:T(8,128)} %param.4) | copy-start | bytes 98308
  0.0 12.3 %copy-start = (f32[256,4096]{1,0:T(8,128)S(1)}, f32[256,4096]{1,0:T(8,128)}, u32[]{:S(2)}) copy-start(f32[256,4096]{1,0:T(8,128)} %values.1) | copy-start | bytes 12582916
  52.0 47.6 %copy-start.2 = (f32[32]{0:T(128)S(1)}, f32[32]{0:T(128)}, u32[]{:S(2)}) copy-start(f32[32]{0:T(128)} %param.5) | copy-start | bytes 388

commit v7 on v6

--- a/solution.py
+++ b/solution.py
@@ -42,7 +42,7 @@
     for c in range(0, GROUPS, 2):
         for pair in zip(*CORE_0_CLASSES):
             first += [
-                [device((2 * far - odd) % DEPTH, x, y, c) for x in pair for odd in range(2)]
+                [device(2 * far + odd, x, y, c) for x in pair for odd in range(2)]
                 for far in range(FAR)
                 for y in range(PAIR)
             ]

time: 101 us -> 101 us (level)
  no operation moved by 1% of the time
where the time goes in v7:
time: 101 us; the launch traced here: 100 us
  blocking collectives  95 us (94%)
  Pallas kernels  5.31 us (5%)
    all_to_all x3, blocking collectives, exchanged(): lax.all_to_all(parts, ALL, split_axis=0, concat_axis=0, tiled=True, axis_...  84.7 us
    all_gather x1, blocking collectives, shards(): arrived = lax.all_gather(own_queries(mask, events, keep_rate[None]), 'cols')  10.3 us
    pallas_call x1, Pallas kernels, local_gram(): pl.pallas_call(gram_kernel, in_specs=[whole, whole, whole], out_specs=who...  2.24 us

profile of v7, /device:TPU:16, one launch (start us, length us, event | category | flops | bytes accessed | tf_op | source)
XLA Modules:
  0.0 100.4 jit_solution(9638615851336785837)
XLA Ops:
  0.0 0.0 copy-start.1
  0.0 0.0 copy-start
  0.0 1.9 %queries.1 = f32[72,256]{1,0:T(8,128)} custom-call(s32[32,256]{1,0:T(8,128)} %bitcast.5, f32[256,4096]{1,0:T(8,128)} %values.1, f32[1,32]{1,0:T(1,128)} %bitcast.7), custom_call_target="tpu_custom_call" | custom-call | flops 16777216 | bytes 262144 | tf_op jit(solution)/shard_map/queries/pallas_call | solution.py:107
  1.9 10.3 %all-gather = f32[288,256]{1,0:T(8,128)S(1)} all-gather(f32[72,256]{1,0:T(8,128)} %queries.1), channel_id=2, replica_groups=mesh['z'=16,'x'=4,'y'=2,'cols'=4] {'cols'}, dimensions={0}, use_global_device_ids=true | all-gather | bytes 368640 | tf_op jit(solution)/shard_map/all_gather | solution.py:327
  12.3 0.0 copy-done.1
  12.3 0.0 copy-done
  12.3 2.2 %gram.1 = f32[4,2088,128]{2,1,0:T(8,128)S(1)} custom-call(f32[4,72,256]{2,1,0:T(8,128)S(1)} %bitcast.3, s32[32,256]{1,0:T(8,128)S(1)} %bitcast.6, f32[256,4096]{1,0:T(8,128)S(1)} %copy-done), custom_call_target="tpu_custom_call" | custom-call | flops 1610612736 | bytes 8388608 | tf_op jit(solution)/shard_map/gram/pallas_call | solution.py:185
  14.5 29.9 %all_to_all.15.arrived = f32[4,2088,128]{2,1,0:T(8,128)S(1)} all-to-all(f32[4,2088,128]{2,1,0:T(8,128)S(1)} %gram.1), channel_id=1, replica_groups={{0,32,8,40},{4,36,12,44},{64,96,72,104},{68,100,76,108},{128,160,136,16..., dimensions={0} | all-to-all | bytes 8552448 | tf_op jit(solution)/shard_map/all_to_all | solution.py:205
  44.4 0.0 copy-start.2
  44.4 0.2 first_sum.1
  44.6 14.2 %all_to_all.16.arrived = f32[4,552,128]{2,1,0:T(8,128)S(1)} all-to-all(f32[4,552,128]{2,1,0:T(8,128)S(1)} %first_sum.1), channel_id=1, replica_groups={{0,4,24,28},{32,36,56,60},{64,68,88,92},{96,100,120,124},{128,132,152,1..., dimensions={0} | all-to-all | bytes 2260992 | tf_op jit(solution)/shard_map/all_to_all | solution.py:205
  58.8 0.2 second_sum.1
  59.0 40.6 %all_to_all.17.arrived = f32[8,104,128]{2,1,0:T(8,128)S(1)} all-to-all(f32[8,104,128]{2,1,0:T(8,128)S(1)} %second_sum.1), channel_id=1, replica_groups={{0,64,128,192,256,320,384,448},{1,65,129,193,257,321,385,449},{2,66,130..., dimensions={0} | all-to-all | bytes 851968 | tf_op jit(solution)/shard_map/all_to_all | solution.py:205
  99.6 0.0 copy-done.2
  99.6 0.1 broadcast_in_dim.10.rates
  99.6 0.8 last_sum.1
Async XLA Ops:
  0.0 12.3 %copy-start.1 = (s32[256,32]{0,1:T(8,128)S(1)}, s32[256,32]{0,1:T(8,128)}, u32[]{:S(2)}) copy-start(s32[256,32]{0,1:T(8,128)} %param.4) | copy-start | bytes 98308
  0.0 12.3 %copy-start = (f32[256,4096]{1,0:T(8,128)S(1)}, f32[256,4096]{1,0:T(8,128)}, u32[]{:S(2)}) copy-start(f32[256,4096]{1,0:T(8,128)} %values.1) | copy-start | bytes 12582916
  44.4 55.1 %copy-start.2 = (f32[32]{0:T(128)S(1)}, f32[32]{0:T(128)}, u32[]{:S(2)}) copy-start(f32[32]{0:T(128)} %param.5) | copy-start | bytes 388

commit v8 on v5

--- a/solution.py
+++ b/solution.py
@@ -238,14 +238,18 @@
     blocks = rows // each
     for place in range(FAR):
         for query in range(share):
-            total[place, query * blocks : (query + 1) * blocks, :] = whole[
-                pl.ds(place * share + query, blocks, stride=each), :
-            ]
-        total[place, share * blocks :, :] = value[rows:]
+            for k in range(blocks // 2):
+                first = place * share + query + 2 * k * each
+                total[place, query * blocks // 2 + k] = whole[pl.ds(first, 2, stride=each), :]
+        last = share * blocks // 2
+        for k in range(total.shape[1] - last):
+            total[place, last + k] = value[rows + 2 * k : rows + 2 * k + 2]
 
 
 def second_sum(arrived):
-    shape = (FAR, (arrived.shape[1] - EXTRA) // FAR + EXTRA, BLOCK)
+    rows = arrived.shape[1] - EXTRA
+    sums = rows * FAN * FAN // QUERIES + QUERIES // BLOCK
+    shape = (FAR, (rows // FAR + sums) // 2, 2, BLOCK)
     return pl.pallas_call(
         second_sum_kernel,
         out_shape=jax.ShapeDtypeStruct(shape, jnp.float32),
@@ -263,41 +267,36 @@
     for sender in range(1, FAR):
         total += arrived[sender]
     share, columns = similarity.shape
-    blocks = columns // BLOCK
-    squares = total[share * blocks : (share + 1) * blocks]
-    weight = lax.rsqrt(squares * rates[...] + EPSILON) * factor
+    half = columns // BLOCK // 2
+    squares = total[share * half : (share + 1) * half]
+    paired = jnp.stack([rates[2 * k : 2 * k + 2, :] for k in range(half)])
+    weight = lax.rsqrt(squares * paired + EPSILON) * factor
 
     z, x, y = (lax.axis_index(a) for a in ROWS)
     mine = ((x * FAN + y * 2 + z % 2) * FAR + z // 2) * share
     group = z // (DEPTH // GROUPS)
-    query_squares = total[(share + 1) * blocks : (share + 1) * blocks + QUERIES // BLOCK]
+    query_squares = total[(share + 1) * half]
     row = lax.broadcasted_iota(jnp.int32, query_squares.shape, 0)
     lane = lax.broadcasted_iota(jnp.int32, query_squares.shape, 1)
-    query_rate = queries[0, 1:2, :1]
+    at = QUERY_GROUP + 1
+    query_rate = queries[0, at : at + 1, :1]
     for k in range(1, GROUPS):
-        query_rate = jnp.where(group == k, queries[k, 1:2, :1], query_rate)
+        query_rate = jnp.where(group == k, queries[k, at : at + 1, :1], query_rate)
     for query in range(share):
         found = jnp.where(row * BLOCK + lane == mine + query, query_squares, 0.0)
         found = jnp.sum(jnp.sum(found, axis=1, keepdims=True), axis=0, keepdims=True)
         scale = lax.rsqrt(found * query_rate + EPSILON)
-        result = total[query * blocks : (query + 1) * blocks] * weight * scale
-        for b in range(blocks):
-            similarity[query : query + 1, b * BLOCK : (b + 1) * BLOCK] = result[b : b + 1]
+        result = total[query * half : (query + 1) * half] * weight * scale[None]
+        for b in range(2 * half):
+            similarity[query : query + 1, b * BLOCK : (b + 1) * BLOCK] = result[
+                b // 2, b % 2 : b % 2 + 1
+            ]
 
 
 def last_sum(factor, arrived, queries, rates):
-    blocks, share = rates.shape[0], QUERIES // (FAN * FAN * FAR)
-    shape = (share, blocks * BLOCK)
-    whole = lambda a: pl.BlockSpec(a.shape, lambda i: (0,) * a.ndim)
+    shape = (QUERIES // (FAN * FAN * FAR), rates.shape[0] * BLOCK)
     return pl.pallas_call(
         functools.partial(last_sum_kernel, factor),
-        grid=(1,),
-        in_specs=[
-            whole(arrived),
-            pl.BlockSpec((GROUPS, 8, queries.shape[2]), lambda i: (0, QUERY_GROUP // 8, 0)),
-            whole(rates),
-        ],
-        out_specs=pl.BlockSpec(shape, lambda i: (0, 0)),
         out_shape=jax.ShapeDtypeStruct(shape, jnp.float32),
         compiler_params=pltpu.CompilerParams(vmem_limit_bytes=32 << 20),
         cost_estimate=pl.CostEstimate(

time: 100 us -> 99 us (0.990)
  blocking collectives: 94.3 us -> 93.3 us
    all_to_all x3, blocking collectives: 84 us -> 83 us  [exchanged(): lax.all_to_all(parts, ALL, split_axis=0, concat_axis=0, tiled=True, axis_...]
where the time goes in v8:
time: 99 us; the launch traced here: 98.8 us
  blocking collectives  93.3 us (94%)
  Pallas kernels  5.37 us (5%)
    all_to_all x3, blocking collectives, exchanged(): lax.all_to_all(parts, ALL, split_axis=0, concat_axis=0, tiled=True, axis_...  83 us
    all_gather x1, blocking collectives, shards(): arrived = lax.all_gather(own_queries(mask, events, keep_rate[None]), 'cols')  10.3 us
    pallas_call x1, Pallas kernels, local_gram(): pl.pallas_call(gram_kernel, in_specs=[whole, whole, whole], out_specs=who...  2.24 us

profile of v8, /device:TPU:16, one launch (start us, length us, event | category | flops | bytes accessed | tf_op | source)
XLA Modules:
  0.0 98.8 jit_solution(3312064686900574821)
XLA Ops:
  0.0 0.0 copy-start.1
  0.0 0.0 copy-start
  0.0 1.9 %queries.1 = f32[72,256]{1,0:T(8,128)} custom-call(s32[32,256]{1,0:T(8,128)} %bitcast.5, f32[256,4096]{1,0:T(8,128)} %values.1, f32[1,32]{1,0:T(1,128)} %bitcast.7), custom_call_target="tpu_custom_call" | custom-call | flops 16777216 | bytes 262144 | tf_op jit(solution)/shard_map/queries/pallas_call | solution.py:97
  1.9 10.3 %all-gather = f32[288,256]{1,0:T(8,128)S(1)} all-gather(f32[72,256]{1,0:T(8,128)} %queries.1), channel_id=2, replica_groups=mesh['z'=16,'x'=4,'y'=2,'cols'=4] {'cols'}, dimensions={0}, use_global_device_ids=true | all-gather | bytes 368640 | tf_op jit(solution)/shard_map/all_gather | solution.py:312
  12.3 0.0 copy-done.1
  12.3 0.0 copy-done
  12.3 2.2 %gram.1 = f32[4,2088,128]{2,1,0:T(8,128)S(1)} custom-call(f32[4,72,256]{2,1,0:T(8,128)S(1)} %bitcast.3, s32[32,256]{1,0:T(8,128)S(1)} %bitcast.6, f32[256,4096]{1,0:T(8,128)S(1)} %copy-done), custom_call_target="tpu_custom_call" | custom-call | flops 1610612736 | bytes 8388608 | tf_op jit(solution)/shard_map/gram/pallas_call | solution.py:171
  14.5 30.7 %all_to_all.15.arrived = f32[4,2088,128]{2,1,0:T(8,128)S(1)} all-to-all(f32[4,2088,128]{2,1,0:T(8,128)S(1)} %gram.1), channel_id=1, replica_groups={{0,8,16,24},{4,12,20,28},{32,40,48,56},{36,44,52,60},{64,72,80,88},{68,..., dimensions={0} | all-to-all | bytes 8552448 | tf_op jit(solution)/shard_map/all_to_all | solution.py:191
  45.3 0.0 copy-start.2
  45.3 0.2 first_sum.1
  45.5 13.0 %all_to_all.16.arrived = f32[4,552,128]{2,1,0:T(8,128)S(1)} all-to-all(f32[4,552,128]{2,1,0:T(8,128)S(1)} %first_sum.1), channel_id=1, replica_groups={{0,32,4,36},{8,40,12,44},{16,48,20,52},{24,56,28,60},{64,96,68,100},{72..., dimensions={0} | all-to-all | bytes 2260992 | tf_op jit(solution)/shard_map/all_to_all | solution.py:191
  58.4 0.2 second_sum.1
  58.6 39.3 %all_to_all.17.arrived = f32[8,49,2,128]{3,2,1,0:T(2,128)S(1)} all-to-all(f32[8,49,2,128]{3,2,1,0:T(2,128)S(1)} %second_sum.1), channel_id=1, replica_groups={{0,64,128,192,256,320,384,448},{1,65,129,193,257,321,385,449},{2,66,130..., dimensions={0} | all-to-all | bytes 802816 | tf_op jit(solution)/shard_map/all_to_all | solution.py:191
  97.9 0.0 copy-done.2
  97.9 0.1 broadcast_in_dim.10.rates
  98.0 0.8 last_sum.1
Async XLA Ops:
  0.0 12.3 %copy-start.1 = (s32[256,32]{0,1:T(8,128)S(1)}, s32[256,32]{0,1:T(8,128)}, u32[]{:S(2)}) copy-start(s32[256,32]{0,1:T(8,128)} %param.4) | copy-start | bytes 98308
  0.0 12.3 %copy-start = (f32[256,4096]{1,0:T(8,128)S(1)}, f32[256,4096]{1,0:T(8,128)}, u32[]{:S(2)}) copy-start(f32[256,4096]{1,0:T(8,128)} %values.1) | copy-start | bytes 12582916
  45.3 52.6 %copy-start.2 = (f32[32]{0:T(128)S(1)}, f32[32]{0:T(128)}, u32[]{:S(2)}) copy-start(f32[32]{0:T(128)} %param.5) | copy-start | bytes 388

commit v9 on v8

--- a/solution.py
+++ b/solution.py
@@ -77,15 +77,33 @@
     )
 
 
-def query_kernel(mask, events, rate, sent):
-    rows = events.shape[0]
+def query_kernel(mask, events, rate, sent, keeps, near, rates, come):
+    copies = (
+        pltpu.make_async_copy(events.at[:, pl.ds(0, BLOCK)], near, come.at[0]),
+        pltpu.make_async_copy(mask.at[pl.ds(0, 8)], keeps, come.at[1]),
+        pltpu.make_async_copy(rate, rates, come.at[2]),
+    )
+    for copy in copies:
+        copy.start()
+    rows = near.shape[0]
     n = lax.broadcasted_iota(jnp.int32, (QUERY_GROUP, BLOCK), 0)
     column = lax.broadcasted_iota(jnp.int32, (QUERY_GROUP, BLOCK), 1)
     x, y, low, next_, query = n >> 4, (n >> 3) & 1, (n >> 2) & 1, (n >> 1) & 1, n & 1
     source = (next_ * 2 + low) * 16 + x * 4 + y * 2 + query
-    sent[:QUERY_GROUP, :] = turned((column == source).astype(jnp.float32), events[...])
-    keep = mask[:1, :].astype(jnp.float32)
-    scale = jnp.broadcast_to(rate[:, :1], (1, rows))
+    pick = (column == source).astype(jnp.float32).astype(jnp.bfloat16)
+    for copy in copies:
+        copy.wait()
+    rest, total = near[...], None
+    for _ in range(3):
+        part = rest.astype(jnp.bfloat16)
+        rest = rest - part.astype(jnp.float32)
+        chosen = lax.dot_general(
+            pick, part, (((1,), (1,)), ((), ())), preferred_element_type=jnp.float32
+        )
+        total = chosen if total is None else total + chosen
+    sent[:QUERY_GROUP, :] = total
+    keep = keeps[:1, :].astype(jnp.float32)
+    scale = jnp.broadcast_to(rates[:, :1], (1, rows))
     sent[QUERY_GROUP:, :] = jnp.concatenate(
         [keep, scale, jnp.zeros((6, rows), jnp.float32)], axis=0
     )
@@ -93,17 +111,17 @@
 
 def own_queries(mask, events, rate):
     rows = events.shape[0]
-    shape = (QUERY_GROUP + 8, rows)
+    there = pl.BlockSpec(memory_space=pl.ANY)
     return pl.pallas_call(
         query_kernel,
-        grid=(1,),
-        in_specs=[
-            pl.BlockSpec((8, rows), lambda i: (0, 0)),
-            pl.BlockSpec((rows, BLOCK), lambda i: (0, 0)),
-            pl.BlockSpec(rate.shape, lambda i: (0, 0)),
+        in_specs=[there] * 3,
+        out_shape=jax.ShapeDtypeStruct((QUERY_GROUP + 8, rows), jnp.float32),
+        scratch_shapes=[
+            pltpu.VMEM((8, rows), mask.dtype),
+            pltpu.VMEM((rows, BLOCK), events.dtype),
+            pltpu.VMEM(rate.shape, rate.dtype),
+            pltpu.SemaphoreType.DMA((3,)),
         ],
-        out_specs=pl.BlockSpec(shape, lambda i: (0, 0)),
-        out_shape=jax.ShapeDtypeStruct(shape, jnp.float32),
         compiler_params=pltpu.CompilerParams(vmem_limit_bytes=56 << 20),
         cost_estimate=pl.CostEstimate(flops=1 << 24, bytes_accessed=1 << 18, transcendentals=0),
         name="queries",

time: 99 us -> 99 us (level)
  no operation moved by 1% of the time
where the time goes in v9:
time: 99 us; the launch traced here: 98.8 us
  blocking collectives  93.3 us (94%)
  Pallas kernels  5.36 us (5%)
    all_to_all x3, blocking collectives, exchanged(): lax.all_to_all(parts, ALL, split_axis=0, concat_axis=0, tiled=True, axis_...  83 us
    all_gather x1, blocking collectives, shards(): arrived = lax.all_gather(own_queries(mask, events, keep_rate[None]), 'cols')  10.4 us
    pallas_call x1, Pallas kernels, local_gram(): pl.pallas_call(gram_kernel, in_specs=[whole, whole, whole], out_specs=who...  2.24 us

profile of v9, /device:TPU:16, one launch (start us, length us, event | category | flops | bytes accessed | tf_op | source)
XLA Modules:
  0.0 98.8 jit_solution(14736001568008321381)
XLA Ops:
  0.0 0.0 copy-start.1
  0.0 0.0 copy-start
  0.0 1.9 %queries.1 = f32[72,256]{1,0:T(8,128)} custom-call(s32[32,256]{1,0:T(8,128)} %bitcast.5, f32[256,4096]{1,0:T(8,128)} %values.1, f32[1,32]{1,0:T(1,128)} %bitcast.7), custom_call_target="tpu_custom_call" | custom-call | flops 16777216 | bytes 262144 | tf_op jit(solution)/shard_map/queries/pallas_call | solution.py:115
  1.9 10.4 %all-gather = f32[288,256]{1,0:T(8,128)S(1)} all-gather(f32[72,256]{1,0:T(8,128)} %queries.1), channel_id=2, replica_groups=mesh['z'=16,'x'=4,'y'=2,'cols'=4] {'cols'}, dimensions={0}, use_global_device_ids=true | all-gather | bytes 368640 | tf_op jit(solution)/shard_map/all_gather | solution.py:330
  12.3 0.0 copy-done.1
  12.3 0.0 copy-done
  12.3 2.2 %gram.1 = f32[4,2088,128]{2,1,0:T(8,128)S(1)} custom-call(f32[4,72,256]{2,1,0:T(8,128)S(1)} %bitcast.3, s32[32,256]{1,0:T(8,128)S(1)} %bitcast.6, f32[256,4096]{1,0:T(8,128)S(1)} %copy-done), custom_call_target="tpu_custom_call" | custom-call | flops 1610612736 | bytes 8388608 | tf_op jit(solution)/shard_map/gram/pallas_call | solution.py:189
  14.5 30.7 %all_to_all.15.arrived = f32[4,2088,128]{2,1,0:T(8,128)S(1)} all-to-all(f32[4,2088,128]{2,1,0:T(8,128)S(1)} %gram.1), channel_id=1, replica_groups={{0,8,16,24},{4,12,20,28},{32,40,48,56},{36,44,52,60},{64,72,80,88},{68,..., dimensions={0} | all-to-all | bytes 8552448 | tf_op jit(solution)/shard_map/all_to_all | solution.py:209
  45.3 0.0 copy-start.2
  45.3 0.2 first_sum.1
  45.5 13.0 %all_to_all.16.arrived = f32[4,552,128]{2,1,0:T(8,128)S(1)} all-to-all(f32[4,552,128]{2,1,0:T(8,128)S(1)} %first_sum.1), channel_id=1, replica_groups={{0,32,4,36},{8,40,12,44},{16,48,20,52},{24,56,28,60},{64,96,68,100},{72..., dimensions={0} | all-to-all | bytes 2260992 | tf_op jit(solution)/shard_map/all_to_all | solution.py:209
  58.5 0.2 second_sum.1
  58.7 39.2 %all_to_all.17.arrived = f32[8,49,2,128]{3,2,1,0:T(2,128)S(1)} all-to-all(f32[8,49,2,128]{3,2,1,0:T(2,128)S(1)} %second_sum.1), channel_id=1, replica_groups={{0,64,128,192,256,320,384,448},{1,65,129,193,257,321,385,449},{2,66,130..., dimensions={0} | all-to-all | bytes 802816 | tf_op jit(solution)/shard_map/all_to_all | solution.py:209
  97.9 0.0 copy-done.2
  97.9 0.1 broadcast_in_dim.10.rates
  98.0 0.8 last_sum.1
Async XLA Ops:
  0.0 12.3 %copy-start.1 = (s32[256,32]{0,1:T(8,128)S(1)}, s32[256,32]{0,1:T(8,128)}, u32[]{:S(2)}) copy-start(s32[256,32]{0,1:T(8,128)} %param.4) | copy-start | bytes 98308
  0.0 12.3 %copy-start = (f32[256,4096]{1,0:T(8,128)S(1)}, f32[256,4096]{1,0:T(8,128)}, u32[]{:S(2)}) copy-start(f32[256,4096]{1,0:T(8,128)} %values.1) | copy-start | bytes 12582916
  45.3 52.6 %copy-start.2 = (f32[32]{0:T(128)S(1)}, f32[32]{0:T(128)}, u32[]{:S(2)}) copy-start(f32[32]{0:T(128)} %param.5) | copy-start | bytes 388

commit v10 on v9

--- a/solution.py
+++ b/solution.py
@@ -65,16 +65,6 @@
     high = values.astype(jnp.bfloat16)
     low = (values - high.astype(jnp.float32)).astype(jnp.bfloat16)
     return high, low
-
-
-def turned(left, right):
-    return lax.dot_general(
-        left,
-        right,
-        (((1,), (1,)), ((), ())),
-        precision=lax.Precision.HIGHEST,
-        preferred_element_type=jnp.float32,
-    )
 
 
 def query_kernel(mask, events, rate, sent, keeps, near, rates, come):
@@ -150,7 +140,17 @@
         high[pl.ds(at, run * GROUPS), :] = h
         low[pl.ds(at, run * GROUPS), :] = l
     raw = jnp.concatenate(raw, axis=0)
-    sums = turned(jnp.ones((8, rows), jnp.float32), raw * raw)[:1]
+    rest, sums = raw * raw, None
+    for _ in range(3):
+        part = rest.astype(jnp.bfloat16)
+        rest = rest - part.astype(jnp.float32)
+        added = lax.dot_general(
+            jnp.ones((8, rows), jnp.bfloat16),
+            part,
+            (((1,), (1,)), ((), ())),
+            preferred_element_type=jnp.float32,
+        )[:1]
+        sums = added if sums is None else sums + added
     last = [sums[:, k : k + BLOCK] for k in range(0, QUERIES, BLOCK)]
     last.append(jnp.zeros((EXTRA - blocks - len(last), BLOCK), jnp.float32))
     last = jnp.concatenate(last, axis=0)

time: 99 us -> 98.8 us (level)
  no operation moved by 1% of the time
where the time goes in v10:
time: 98.8 us; the launch traced here: 98.6 us
  blocking collectives  93.3 us (94%)
  Pallas kernels  5.21 us (5%)
    all_to_all x3, blocking collectives, exchanged(): lax.all_to_all(parts, ALL, split_axis=0, concat_axis=0, tiled=True, axis_...  83 us
    all_gather x1, blocking collectives, shards(): arrived = lax.all_gather(own_queries(mask, events, keep_rate[None]), 'cols')  10.4 us
    pallas_call x1, Pallas kernels, local_gram(): pl.pallas_call(gram_kernel, in_specs=[whole, whole, whole], out_specs=who...  2.09 us

profile of v10, /device:TPU:16, one launch (start us, length us, event | category | flops | bytes accessed | tf_op | source)
XLA Modules:
  0.0 98.6 jit_solution(9065466981412905550)
XLA Ops:
  0.0 0.0 copy-start.1
  0.0 0.0 copy-start
  0.0 1.9 %queries.1 = f32[72,256]{1,0:T(8,128)} custom-call(s32[32,256]{1,0:T(8,128)} %bitcast.5, f32[256,4096]{1,0:T(8,128)} %values.1, f32[1,32]{1,0:T(1,128)} %bitcast.7), custom_call_target="tpu_custom_call" | custom-call | flops 16777216 | bytes 262144 | tf_op jit(solution)/shard_map/queries/pallas_call | solution.py:105
  1.9 10.4 %all-gather = f32[288,256]{1,0:T(8,128)S(1)} all-gather(f32[72,256]{1,0:T(8,128)} %queries.1), channel_id=2, replica_groups=mesh['z'=16,'x'=4,'y'=2,'cols'=4] {'cols'}, dimensions={0}, use_global_device_ids=true | all-gather | bytes 368640 | tf_op jit(solution)/shard_map/all_gather | solution.py:330
  12.3 0.0 copy-done.1
  12.3 0.0 copy-done
  12.3 2.1 %gram.1 = f32[4,2088,128]{2,1,0:T(8,128)S(1)} custom-call(f32[4,72,256]{2,1,0:T(8,128)S(1)} %bitcast.3, s32[32,256]{1,0:T(8,128)S(1)} %bitcast.6, f32[256,4096]{1,0:T(8,128)S(1)} %copy-done), custom_call_target="tpu_custom_call" | custom-call | flops 1610612736 | bytes 8388608 | tf_op jit(solution)/shard_map/gram/pallas_call | solution.py:189
  14.4 30.7 %all_to_all.15.arrived = f32[4,2088,128]{2,1,0:T(8,128)S(1)} all-to-all(f32[4,2088,128]{2,1,0:T(8,128)S(1)} %gram.1), channel_id=1, replica_groups={{0,8,16,24},{4,12,20,28},{32,40,48,56},{36,44,52,60},{64,72,80,88},{68,..., dimensions={0} | all-to-all | bytes 8552448 | tf_op jit(solution)/shard_map/all_to_all | solution.py:209
  45.1 0.0 copy-start.2
  45.1 0.2 first_sum.1
  45.3 13.0 %all_to_all.16.arrived = f32[4,552,128]{2,1,0:T(8,128)S(1)} all-to-all(f32[4,552,128]{2,1,0:T(8,128)S(1)} %first_sum.1), channel_id=1, replica_groups={{0,32,4,36},{8,40,12,44},{16,48,20,52},{24,56,28,60},{64,96,68,100},{72..., dimensions={0} | all-to-all | bytes 2260992 | tf_op jit(solution)/shard_map/all_to_all | solution.py:209
  58.3 0.2 second_sum.1
  58.5 39.2 %all_to_all.17.arrived = f32[8,49,2,128]{3,2,1,0:T(2,128)S(1)} all-to-all(f32[8,49,2,128]{3,2,1,0:T(2,128)S(1)} %second_sum.1), channel_id=1, replica_groups={{0,64,128,192,256,320,384,448},{1,65,129,193,257,321,385,449},{2,66,130..., dimensions={0} | all-to-all | bytes 802816 | tf_op jit(solution)/shard_map/all_to_all | solution.py:209
  97.8 0.0 copy-done.2
  97.8 0.1 broadcast_in_dim.10.rates
  97.8 0.8 last_sum.1
Async XLA Ops:
  0.0 12.3 %copy-start.1 = (s32[256,32]{0,1:T(8,128)S(1)}, s32[256,32]{0,1:T(8,128)}, u32[]{:S(2)}) copy-start(s32[256,32]{0,1:T(8,128)} %param.4) | copy-start | bytes 98308
  0.0 12.3 %copy-start = (f32[256,4096]{1,0:T(8,128)S(1)}, f32[256,4096]{1,0:T(8,128)}, u32[]{:S(2)}) copy-start(f32[256,4096]{1,0:T(8,128)} %values.1) | copy-start | bytes 12582916
  45.1 52.6 %copy-start.2 = (f32[32]{0:T(128)S(1)}, f32[32]{0:T(128)}, u32[]{:S(2)}) copy-start(f32[32]{0:T(128)} %param.5) | copy-start | bytes 388
